TPU v7x, 256 devices: a whole 4x4x8 slice. The times are simulated.
256 devices in a mesh: rows: 16 (over y, x), cols: 16 (over z, core).
Axes of the slice: x: 4, y: 4, z: 8, core: 2. Of those that a mesh axis runs over, the one named last changes fastest.
Arguments:
- design: float32 [6, 32, 128], P(None, 'rows', 'cols'), may hold values from -6 to 6
- active: int32 [32, 128], P('rows', 'cols'), may hold values 0 or 1
- stamp_basis: float32 [6, 32, 32], replicated, may hold values from -2 to 2
- film_field: bfloat16 [16, 512, 2048], P(None, 'rows', 'cols'), may hold values from -6 to 6
- lift_weight: float32 [16], replicated, may hold values from -4 to 4
- lift_bias: float32 [16], replicated, may hold values from -3 to 3
- conv_weight: bfloat16 [4, 9, 16, 16], replicated, may hold values from -0.5 to 0.5
- conv_bias: float32 [4, 16], replicated, may hold values from -3 to 3
- readout: float32 [16], replicated, may hold values from -1.5 to 1.5
- target: float32 [512, 2048], P('rows', 'cols'), may hold values from -6 to 6
- dilation: int32 [4], replicated, may hold values from 1 to 8, as said below
Outputs:
- new_design: float32 [6, 32, 128], P(None, 'rows', 'cols')
- objective: float32 [2], replicated
Inputs may be any that keep to these rules, and one draw needn't show every extreme that they name: The dilation of each layer is an integer from 1 to 8; some layer has exactly 8.
All inputs are finite; a program needn't handle non-finite values. No bound on the sum of `active` on one device may be relied on, other than what follows from the above.
Results may differ from a plain program's by a relative error of at most 0.0025.
Values may be sent and summed in bfloat16 or wider, within the bound.
No kernel may reach another device: no remote copies, remote signals or barrier semaphores. Data moves between devices by JAX's collectives and lax.ppermute only.
A program may use at most 64 MiB of HBM per device.

v0:
```python
import jax
import jax.numpy as jnp
from jax import lax
from jax.sharding import PartitionSpec as P

DMAX = 8
LAYERS = 4
ITERS = 2


step_rate = 0.25
norm_eps = 1e-06


def with_halo(array, sides, width):
    for axis, dim in sides:
        count, length = (lax.axis_size(axis), array.shape[dim])
        up = [(i, (i + 1) % count) for i in range(count - 1)]
        down = [(j, i) for i, j in up]
        last = lax.slice_in_dim(array, length - width, length, axis=dim)
        first = lax.slice_in_dim(array, 0, width, axis=dim)
        before = lax.ppermute(last, axis, up)
        after = lax.ppermute(first, axis, down)
        array = jnp.concatenate([before, array, after], axis=dim)
    return array


def tap_list():
    return [(row_step, col_step) for row_step in (-1, 0, 1) for col_step in (-1, 0, 1)]


def basis_blocks(stamp_basis):
    side = stamp_basis.shape[1] // 2
    padded_basis = jnp.pad(stamp_basis, ((0, 0), (side, side), (side, side)))
    pieces = []
    for row_step, col_step in tap_list():
        top = side + side // 2 - side * row_step
        left = side + side // 2 - side * col_step
        pieces.append(padded_basis[:, top : top + side, left : left + side])
    return jnp.stack(pieces)


def render(padded_amp, blocks, dimple_rows, dimple_cols):
    side = blocks.shape[2]
    shifted = jnp.stack(
        [
            padded_amp[:, 1 + r : 1 + r + dimple_rows, 1 + c : 1 + c + dimple_cols]
            for r, c in tap_list()
        ]
    )
    tiles = jnp.einsum("tpab,tpyx->aybx", shifted, blocks, precision=lax.Precision.HIGHEST)
    return tiles.reshape(dimple_rows * side, dimple_cols * side)


def render_back(padded_grad, blocks, dimple_rows, dimple_cols):
    side = blocks.shape[2]
    framed = padded_grad.reshape(dimple_rows + 2, side, dimple_cols + 2, side)
    summed = jnp.zeros((blocks.shape[1], dimple_rows, dimple_cols), jnp.float32)
    for index, (r, c) in enumerate(tap_list()):
        window = framed[1 - r : 1 - r + dimple_rows, :, 1 - c : 1 - c + dimple_cols, :]
        summed = summed + jnp.einsum(
            "aybx,pyx->pab", window, blocks[index], precision=lax.Precision.HIGHEST
        )
    return summed


def conv_forward(padded, weight, bias, dilate, out_rows, out_cols):
    channels = weight.shape[1]
    summed = jnp.zeros((channels, out_rows, out_cols), jnp.float32)
    zero = jnp.asarray(0, jnp.int32)
    for index, (r, c) in enumerate(tap_list()):
        window = lax.dynamic_slice(
            padded, (zero, DMAX + r * dilate, DMAX + c * dilate), (channels, out_rows, out_cols)
        )
        summed = summed + jnp.einsum(
            "oc,chw->ohw", weight[index], window, preferred_element_type=jnp.float32
        )
    return summed + bias[:, None, None]


def conv_back(padded, weight, dilate, out_rows, out_cols):
    channels = weight.shape[1]
    summed = jnp.zeros((channels, out_rows, out_cols), jnp.float32)
    zero = jnp.asarray(0, jnp.int32)
    for index, (r, c) in enumerate(tap_list()):
        window = lax.dynamic_slice(
            padded, (zero, DMAX - r * dilate, DMAX - c * dilate), (channels, out_rows, out_cols)
        )
        summed = summed + jnp.einsum(
            "oc,ohw->chw", weight[index], window, preferred_element_type=jnp.float32
        )
    return summed


def silu_slope(value):
    logistic = jax.nn.sigmoid(value)
    return logistic * (1.0 + value * (1.0 - logistic))


def on_device(
    design,
    active,
    stamp_basis,
    film_field,
    lift_weight,
    lift_bias,
    conv_weight,
    conv_bias,
    readout,
    target,
    dilation,
):
    channels, cell_rows, cell_cols = film_field.shape
    nparams, dimple_rows, dimple_cols = design.shape
    stride = cell_rows // dimple_rows
    row_count = lax.axis_size("rows")
    col_count = lax.axis_size("cols")
    total_cells = cell_rows * cell_cols * row_count * col_count
    total_entries = nparams * dimple_rows * dimple_cols * row_count * col_count
    blocks = basis_blocks(stamp_basis)
    active_mask = active.astype(jnp.float32)
    params = design
    objectives = []
    for iteration in range(ITERS):
        amplitude = params * active_mask
        padded_amp = with_halo(amplitude, (("rows", 1), ("cols", 2)), 1)
        height = render(padded_amp, blocks, dimple_rows, dimple_cols)
        state = (
            lift_weight[:, None, None] * height[None]
            + lift_bias[:, None, None]
            + film_field.astype(jnp.float32)
        ).astype(jnp.bfloat16)
        pres = []
        for layer in range(LAYERS):
            padded = with_halo(state, (("rows", 1), ("cols", 2)), DMAX)
            pre = conv_forward(
                padded, conv_weight[layer], conv_bias[layer], dilation[layer], cell_rows, cell_cols
            )
            pres.append(pre)
            state = (state.astype(jnp.float32) + jax.nn.silu(pre)).astype(jnp.bfloat16)
        pressure = jnp.sum(readout[:, None, None] * state.astype(jnp.float32), axis=0)
        misfit = pressure - target
        local_misfit = 0.5 * jnp.sum(misfit * misfit)
        objectives.append(lax.psum(local_misfit, ("rows", "cols")) / total_cells)
        adjoint = readout[:, None, None] * (misfit / (stride * stride))[None]
        for layer in range(LAYERS - 1, -1, -1):
            slope = (adjoint * silu_slope(pres[layer])).astype(jnp.bfloat16)
            padded = with_halo(slope, (("rows", 1), ("cols", 2)), DMAX)
            adjoint = adjoint + conv_back(
                padded, conv_weight[layer], dilation[layer], cell_rows, cell_cols
            )
        height_grad = jnp.sum(lift_weight[:, None, None] * adjoint, axis=0)
        grad_rim = with_halo(height_grad, (("rows", 0), ("cols", 1)), stride // 2)
        padded_grad = jnp.pad(grad_rim, stride // 2)
        gradient = render_back(padded_grad, blocks, dimple_rows, dimple_cols) * active_mask
        local_squares = jnp.sum(gradient * gradient)
        squares = lax.psum(local_squares, ("rows", "cols"))
        mean_square = squares / total_entries
        params = params - step_rate * gradient / jnp.sqrt(mean_square + norm_eps)
    return (params, jnp.stack(objectives))


def solution(mesh):
    placed = (
        P(None, "rows", "cols"),
        P("rows", "cols"),
        P(),
        P(None, "rows", "cols"),
        P(),
        P(),
        P(),
        P(),
        P(),
        P("rows", "cols"),
        P(),
    )
    return jax.shard_map(
        on_device,
        mesh=mesh,
        in_specs=placed,
        out_specs=(P(None, "rows", "cols"), P()),
        check_vma=False,
    )
```

profile of v0, /device:TPU:1, one launch (start us, length us, event | category | flops | bytes accessed | tf_op | source)
XLA Modules:
  0.0 632.4 jit_solution(4018830423068499955)
XLA Ops:
  10.9 5.2 collective-permute-start.2
  38.3 4.4 collective-permute-done.7
  45.0 4.1 collective-permute-start.8
  59.7 4.4 collective-permute-done.11
  66.5 5.6 collective-permute-start.12
  82.7 4.5 collective-permute-done.15
  89.5 5.5 collective-permute-start.16
  105.6 4.9 collective-permute-done.19
  114.1 5.4 collective-permute-start.20
  130.1 4.7 collective-permute-done.23
  137.4 5.3 collective-permute-start.24
  153.2 4.7 collective-permute-done.27
  160.6 5.4 collective-permute-start.28
  176.5 4.7 collective-permute-done.31
  183.9 4.7 collective-permute-start.32
  199.2 4.9 collective-permute-done.35
  206.6 4.7 collective-permute-start.36
  236.1 85.2 %psum.28 = f32[]{:T(128)} all-reduce(f32[]{:T(128)} %get-tuple-element.178), channel_id=1, replica_groups=mesh['rows'=16,'cols'=16] {'rows','cols'}, use_global_device_ids=true, to_apply=%region_3.4 | all-reduce | flops 1 | bytes 8 | tf_op jit(solution)/shard_map/psum | solution.py:157
  351.7 4.4 collective-permute-done.47
  358.5 5.1 collective-permute-start.48
  374.2 4.4 collective-permute-done.51
  395.3 4.4 collective-permute-done.55
  416.5 5.2 collective-permute-done.59
  424.8 4.0 collective-permute-start.60
  439.4 5.3 collective-permute-done.63
  462.0 5.3 collective-permute-done.67
  469.9 4.0 collective-permute-start.68
  484.5 5.3 collective-permute-done.71
  492.4 4.0 collective-permute-start.72
  507.0 5.6 collective-permute-done.75
  515.1 4.0 collective-permute-start.76
  544.5 84.3 %all-reduce.3 = (f32[]{:T(128)}, f32[]{:T(128)}, f32[]{:T(128)}) all-reduce(f32[]{:T(128)} %get-tuple-element.194, f32[]{:T(128)S(6)} %mul.395, f32[]{:T(128)S(6)} %mul.393), channel_id=1, replica_groups=mesh['rows'=16,'cols'=16] {'rows','cols'}, use_global_device_ids=true, to_apply=%region_7.8 | all-reduce | flops 3 | bytes 24 | tf_op jit(solution)/shard_map/psum | solution.py:157
  (475 shorter events, 293.6 us)
Async XLA Ops:
  2.0 8.8 %collective-permute-start = (f32[6,1,8]{2,0,1:T(8,128)S(1)}, f32[6,1,8]{2,0,1:T(8,128)S(1)}, u32[]{:S(2)}, u32[]{:S(2)}) collective-permute-start(f32[6,1,8]{2,0,1:T(8,128)S(1)} %get-tuple-element.152), channel_id=1, source_target_pairs={{0,16},{16,32},{32,48},{48,64},{64,80},{80,96},{96,112},{112,128},... | collective-permute-start | bytes 584 | tf_op jit(solution)/shard_map/ppermute | solution.py:22
  10.9 7.4 %collective-permute-start.2 = (f32[6,4,1]{2,0,1:T(8,128)S(1)}, f32[6,4,1]{2,0,1:T(8,128)S(1)}, u32[]{:S(2)}, u32[]{:S(2)}) collective-permute-start(f32[6,4,1]{2,0,1:T(8,128)S(1)} %get-tuple-element.145), channel_id=1, source_target_pairs={{0,1},{1,2},{2,3},{3,4},{4,5},{5,6},{6,7},{7,8},{8,9},{9,10},{10,1... | collective-permute-start | bytes 296 | tf_op jit(solution)/shard_map/ppermute | solution.py:22
  24.0 7.9 %collective-permute-start.4 = (bf16[16,8,128]{2,0,1:T(8,128)(2,1)S(1)}, bf16[16,8,128]{2,0,1:T(8,128)(2,1)S(1)}, u32[]{:S(2)}, u32[]{:S(2)}) collective-permute-start(bf16[16,8,128]{2,0,1:T(8,128)(2,1)S(1)} %get-tuple-element.107), channel_id=1, source_target_pairs={{0,16},{16,32},{32,48},{48,64},{64,80},{80,96},{96,112},{112,128},... | collective-permute-start | bytes 98312 | tf_op jit(solution)/shard_map/ppermute | solution.py:22
  32.3 6.0 collective-permute-start.6
  35.7 7.0 %collective-permute-start.7 = (bf16[16,48,8]{2,0,1:T(8,128)(2,1)S(1)}, bf16[16,48,8]{2,0,1:T(8,128)(2,1)S(1)}, u32[]{:S(2)}, u32[]{:S(2)}) collective-permute-start(bf16[16,48,8]{2,0,1:T(8,128)(2,1)S(1)} %get-tuple-element.76), channel_id=1, source_target_pairs={{1,0},{2,1},{3,2},{4,3},{5,4},{6,5},{7,6},{8,7},{9,8},{10,9},{11,1... | collective-permute-start | bytes 36872 | tf_op jit(solution)/shard_map/ppermute | solution.py:23
  45.0 8.0 %collective-permute-start.8 = (bf16[16,8,128]{2,0,1:T(8,128)(2,1)S(1)}, bf16[16,8,128]{2,0,1:T(8,128)(2,1)S(1)}, u32[]{:S(2)}, u32[]{:S(2)}) collective-permute-start(bf16[16,8,128]{2,0,1:T(8,128)(2,1)S(1)} %get-tuple-element.105), channel_id=1, source_target_pairs={{0,16},{16,32},{32,48},{48,64},{64,80},{80,96},{96,112},{112,128},... | collective-permute-start | bytes 98312 | tf_op jit(solution)/shard_map/ppermute | solution.py:22
  57.1 7.0 %collective-permute-start.11 = (bf16[16,48,8]{2,0,1:T(8,128)(2,1)S(1)}, bf16[16,48,8]{2,0,1:T(8,128)(2,1)S(1)}, u32[]{:S(2)}, u32[]{:S(2)}) collective-permute-start(bf16[16,48,8]{2,0,1:T(8,128)(2,1)S(1)} %get-tuple-element.74), channel_id=1, source_target_pairs={{1,0},{2,1},{3,2},{4,3},{5,4},{6,5},{7,6},{8,7},{9,8},{10,9},{11,1... | collective-permute-start | bytes 36872 | tf_op jit(solution)/shard_map/ppermute | solution.py:23
  66.5 9.4 %collective-permute-start.12 = (bf16[16,8,128]{2,0,1:T(8,128)(2,1)S(1)}, bf16[16,8,128]{2,0,1:T(8,128)(2,1)S(1)}, u32[]{:S(2)}, u32[]{:S(2)}) collective-permute-start(bf16[16,8,128]{2,0,1:T(8,128)(2,1)S(1)} %get-tuple-element.103), channel_id=1, source_target_pairs={{0,16},{16,32},{32,48},{48,64},{64,80},{80,96},{96,112},{112,128},... | collective-permute-start | bytes 98312 | tf_op jit(solution)/shard_map/ppermute | solution.py:22
  80.1 7.0 %collective-permute-start.15 = (bf16[16,48,8]{2,0,1:T(8,128)(2,1)S(1)}, bf16[16,48,8]{2,0,1:T(8,128)(2,1)S(1)}, u32[]{:S(2)}, u32[]{:S(2)}) collective-permute-start(bf16[16,48,8]{2,0,1:T(8,128)(2,1)S(1)} %get-tuple-element.72), channel_id=1, source_target_pairs={{1,0},{2,1},{3,2},{4,3},{5,4},{6,5},{7,6},{8,7},{9,8},{10,9},{11,1... | collective-permute-start | bytes 36872 | tf_op jit(solution)/shard_map/ppermute | solution.py:23
  89.5 9.4 %collective-permute-start.16 = (bf16[16,8,128]{2,0,1:T(8,128)(2,1)S(1)}, bf16[16,8,128]{2,0,1:T(8,128)(2,1)S(1)}, u32[]{:S(2)}, u32[]{:S(2)}) collective-permute-start(bf16[16,8,128]{2,0,1:T(8,128)(2,1)S(1)} %get-tuple-element.101), channel_id=1, source_target_pairs={{0,16},{16,32},{32,48},{48,64},{64,80},{80,96},{96,112},{112,128},... | collective-permute-start | bytes 98312 | tf_op jit(solution)/shard_map/ppermute | solution.py:22
  103.0 7.5 %collective-permute-start.19 = (bf16[16,48,8]{2,0,1:T(8,128)(2,1)S(1)}, bf16[16,48,8]{2,0,1:T(8,128)(2,1)S(1)}, u32[]{:S(2)}, u32[]{:S(2)}) collective-permute-start(bf16[16,48,8]{2,0,1:T(8,128)(2,1)S(1)} %get-tuple-element.70), channel_id=1, source_target_pairs={{1,0},{2,1},{3,2},{4,3},{5,4},{6,5},{7,6},{8,7},{9,8},{10,9},{11,1... | collective-permute-start | bytes 36872 | tf_op jit(solution)/shard_map/ppermute | solution.py:23
  114.1 8.6 %collective-permute-start.20 = (bf16[16,8,128]{2,0,1:T(8,128)(2,1)S(1)}, bf16[16,8,128]{2,0,1:T(8,128)(2,1)S(1)}, u32[]{:S(2)}, u32[]{:S(2)}) collective-permute-start(bf16[16,8,128]{2,0,1:T(8,128)(2,1)S(1)} %get-tuple-element.99), channel_id=1, source_target_pairs={{0,16},{16,32},{32,48},{48,64},{64,80},{80,96},{96,112},{112,128},... | collective-permute-start | bytes 98312 | tf_op jit(solution)/shard_map/ppermute | solution.py:22
  124.3 5.8 collective-permute-start.22
  127.4 7.3 %collective-permute-start.23 = (bf16[16,48,8]{2,0,1:T(8,128)(2,1)S(1)}, bf16[16,48,8]{2,0,1:T(8,128)(2,1)S(1)}, u32[]{:S(2)}, u32[]{:S(2)}) collective-permute-start(bf16[16,48,8]{2,0,1:T(8,128)(2,1)S(1)} %get-tuple-element.68), channel_id=1, source_target_pairs={{1,0},{2,1},{3,2},{4,3},{5,4},{6,5},{7,6},{8,7},{9,8},{10,9},{11,1... | collective-permute-start | bytes 36872 | tf_op jit(solution)/shard_map/ppermute | solution.py:23
  137.4 8.5 %collective-permute-start.24 = (bf16[16,8,128]{2,0,1:T(8,128)(2,1)S(1)}, bf16[16,8,128]{2,0,1:T(8,128)(2,1)S(1)}, u32[]{:S(2)}, u32[]{:S(2)}) collective-permute-start(bf16[16,8,128]{2,0,1:T(8,128)(2,1)S(1)} %get-tuple-element.97), channel_id=1, source_target_pairs={{0,16},{16,32},{32,48},{48,64},{64,80},{80,96},{96,112},{112,128},... | collective-permute-start | bytes 98312 | tf_op jit(solution)/shard_map/ppermute | solution.py:22
  150.6 7.3 %collective-permute-start.27 = (bf16[16,48,8]{2,0,1:T(8,128)(2,1)S(1)}, bf16[16,48,8]{2,0,1:T(8,128)(2,1)S(1)}, u32[]{:S(2)}, u32[]{:S(2)}) collective-permute-start(bf16[16,48,8]{2,0,1:T(8,128)(2,1)S(1)} %get-tuple-element.66), channel_id=1, source_target_pairs={{1,0},{2,1},{3,2},{4,3},{5,4},{6,5},{7,6},{8,7},{9,8},{10,9},{11,1... | collective-permute-start | bytes 36872 | tf_op jit(solution)/shard_map/ppermute | solution.py:23
  160.6 8.6 %collective-permute-start.28 = (bf16[16,8,128]{2,0,1:T(8,128)(2,1)S(1)}, bf16[16,8,128]{2,0,1:T(8,128)(2,1)S(1)}, u32[]{:S(2)}, u32[]{:S(2)}) collective-permute-start(bf16[16,8,128]{2,0,1:T(8,128)(2,1)S(1)} %get-tuple-element.95), channel_id=1, source_target_pairs={{0,16},{16,32},{32,48},{48,64},{64,80},{80,96},{96,112},{112,128},... | collective-permute-start | bytes 98312 | tf_op jit(solution)/shard_map/ppermute | solution.py:22
  173.9 7.3 %collective-permute-start.31 = (bf16[16,48,8]{2,0,1:T(8,128)(2,1)S(1)}, bf16[16,48,8]{2,0,1:T(8,128)(2,1)S(1)}, u32[]{:S(2)}, u32[]{:S(2)}) collective-permute-start(bf16[16,48,8]{2,0,1:T(8,128)(2,1)S(1)} %get-tuple-element.64), channel_id=1, source_target_pairs={{1,0},{2,1},{3,2},{4,3},{5,4},{6,5},{7,6},{8,7},{9,8},{10,9},{11,1... | collective-permute-start | bytes 36872 | tf_op jit(solution)/shard_map/ppermute | solution.py:23
  183.9 7.9 %collective-permute-start.32 = (bf16[16,8,128]{2,0,1:T(8,128)(2,1)S(1)}, bf16[16,8,128]{2,0,1:T(8,128)(2,1)S(1)}, u32[]{:S(2)}, u32[]{:S(2)}) collective-permute-start(bf16[16,8,128]{2,0,1:T(8,128)(2,1)S(1)} %get-tuple-element.93), channel_id=1, source_target_pairs={{0,16},{16,32},{32,48},{48,64},{64,80},{80,96},{96,112},{112,128},... | collective-permute-start | bytes 98312 | tf_op jit(solution)/shard_map/ppermute | solution.py:22
  196.6 7.5 %collective-permute-start.35 = (bf16[16,48,8]{2,0,1:T(8,128)(2,1)S(1)}, bf16[16,48,8]{2,0,1:T(8,128)(2,1)S(1)}, u32[]{:S(2)}, u32[]{:S(2)}) collective-permute-start(bf16[16,48,8]{2,0,1:T(8,128)(2,1)S(1)} %get-tuple-element.62), channel_id=1, source_target_pairs={{1,0},{2,1},{3,2},{4,3},{5,4},{6,5},{7,6},{8,7},{9,8},{10,9},{11,1... | collective-permute-start | bytes 36872 | tf_op jit(solution)/shard_map/ppermute | solution.py:23
  206.6 6.0 collective-permute-start.36
  349.1 7.0 %collective-permute-start.47 = (bf16[16,48,8]{2,0,1:T(8,128)(2,1)S(1)}, bf16[16,48,8]{2,0,1:T(8,128)(2,1)S(1)}, u32[]{:S(2)}, u32[]{:S(2)}) collective-permute-start(bf16[16,48,8]{2,0,1:T(8,128)(2,1)S(1)} %get-tuple-element.60), channel_id=1, source_target_pairs={{1,0},{2,1},{3,2},{4,3},{5,4},{6,5},{7,6},{8,7},{9,8},{10,9},{11,1... | collective-permute-start | bytes 36872 | tf_op jit(solution)/shard_map/ppermute | solution.py:23
  358.5 6.4 %collective-permute-start.48 = (bf16[16,8,128]{2,0,1:T(8,128)(2,1)S(1)}, bf16[16,8,128]{2,0,1:T(8,128)(2,1)S(1)}, u32[]{:S(2)}, u32[]{:S(2)}) collective-permute-start(bf16[16,8,128]{2,0,1:T(8,128)(2,1)S(1)} %get-tuple-element.89), channel_id=1, source_target_pairs={{0,16},{16,32},{32,48},{48,64},{64,80},{80,96},{96,112},{112,128},... | collective-permute-start | bytes 98312 | tf_op jit(solution)/shard_map/ppermute | solution.py:22
  371.6 7.0 %collective-permute-start.51 = (bf16[16,48,8]{2,0,1:T(8,128)(2,1)S(1)}, bf16[16,48,8]{2,0,1:T(8,128)(2,1)S(1)}, u32[]{:S(2)}, u32[]{:S(2)}) collective-permute-start(bf16[16,48,8]{2,0,1:T(8,128)(2,1)S(1)} %get-tuple-element.58), channel_id=1, source_target_pairs={{1,0},{2,1},{3,2},{4,3},{5,4},{6,5},{7,6},{8,7},{9,8},{10,9},{11,1... | collective-permute-start | bytes 36872 | tf_op jit(solution)/shard_map/ppermute | solution.py:23
  392.8 7.0 %collective-permute-start.55 = (bf16[16,48,8]{2,0,1:T(8,128)(2,1)S(1)}, bf16[16,48,8]{2,0,1:T(8,128)(2,1)S(1)}, u32[]{:S(2)}, u32[]{:S(2)}) collective-permute-start(bf16[16,48,8]{2,0,1:T(8,128)(2,1)S(1)} %get-tuple-element.56), channel_id=1, source_target_pairs={{1,0},{2,1},{3,2},{4,3},{5,4},{6,5},{7,6},{8,7},{9,8},{10,9},{11,1... | collective-permute-start | bytes 36872 | tf_op jit(solution)/shard_map/ppermute | solution.py:23
  413.9 7.8 %collective-permute-start.59 = (bf16[16,48,8]{2,0,1:T(8,128)(2,1)S(1)}, bf16[16,48,8]{2,0,1:T(8,128)(2,1)S(1)}, u32[]{:S(2)}, u32[]{:S(2)}) collective-permute-start(bf16[16,48,8]{2,0,1:T(8,128)(2,1)S(1)} %get-tuple-element.54), channel_id=1, source_target_pairs={{1,0},{2,1},{3,2},{4,3},{5,4},{6,5},{7,6},{8,7},{9,8},{10,9},{11,1... | collective-permute-start | bytes 36872 | tf_op jit(solution)/shard_map/ppermute | solution.py:23
  436.8 7.9 %collective-permute-start.63 = (bf16[16,48,8]{2,0,1:T(8,128)(2,1)S(1)}, bf16[16,48,8]{2,0,1:T(8,128)(2,1)S(1)}, u32[]{:S(2)}, u32[]{:S(2)}) collective-permute-start(bf16[16,48,8]{2,0,1:T(8,128)(2,1)S(1)} %get-tuple-element.52), channel_id=1, source_target_pairs={{1,0},{2,1},{3,2},{4,3},{5,4},{6,5},{7,6},{8,7},{9,8},{10,9},{11,1... | collective-permute-start | bytes 36872 | tf_op jit(solution)/shard_map/ppermute | solution.py:23
  459.4 7.9 %collective-permute-start.67 = (bf16[16,48,8]{2,0,1:T(8,128)(2,1)S(1)}, bf16[16,48,8]{2,0,1:T(8,128)(2,1)S(1)}, u32[]{:S(2)}, u32[]{:S(2)}) collective-permute-start(bf16[16,48,8]{2,0,1:T(8,128)(2,1)S(1)} %get-tuple-element.50), channel_id=1, source_target_pairs={{1,0},{2,1},{3,2},{4,3},{5,4},{6,5},{7,6},{8,7},{9,8},{10,9},{11,1... | collective-permute-start | bytes 36872 | tf_op jit(solution)/shard_map/ppermute | solution.py:23
  481.9 7.9 %collective-permute-start.71 = (bf16[16,48,8]{2,0,1:T(8,128)(2,1)S(1)}, bf16[16,48,8]{2,0,1:T(8,128)(2,1)S(1)}, u32[]{:S(2)}, u32[]{:S(2)}) collective-permute-start(bf16[16,48,8]{2,0,1:T(8,128)(2,1)S(1)} %get-tuple-element.48), channel_id=1, source_target_pairs={{1,0},{2,1},{3,2},{4,3},{5,4},{6,5},{7,6},{8,7},{9,8},{10,9},{11,1... | collective-permute-start | bytes 36872 | tf_op jit(solution)/shard_map/ppermute | solution.py:23
  504.4 8.2 %collective-permute-start.75 = (bf16[16,48,8]{2,0,1:T(8,128)(2,1)S(1)}, bf16[16,48,8]{2,0,1:T(8,128)(2,1)S(1)}, u32[]{:S(2)}, u32[]{:S(2)}) collective-permute-start(bf16[16,48,8]{2,0,1:T(8,128)(2,1)S(1)} %get-tuple-element.46), channel_id=1, source_target_pairs={{1,0},{2,1},{3,2},{4,3},{5,4},{6,5},{7,6},{8,7},{9,8},{10,9},{11,1... | collective-permute-start | bytes 36872 | tf_op jit(solution)/shard_map/ppermute | solution.py:23
  523.6 6.4 %collective-permute-start.78 = (f32[48,8]{1,0:T(8,128)S(1)}, f32[48,8]{1,0:T(8,128)S(1)}, u32[]{:S(2)}, u32[]{:S(2)}) collective-permute-start(f32[48,8]{1,0:T(8,128)S(1)} %get-tuple-element.118), channel_id=1, source_target_pairs={{0,1},{1,2},{2,3},{3,4},{4,5},{5,6},{6,7},{7,8},{8,9},{9,10},{10,1... | collective-permute-start | bytes 4616 | tf_op jit(solution)/shard_map/ppermute | solution.py:22
  526.8 6.1 collective-permute-start.79
  (58 other events, 347.2 us)
where the time goes:
time: 643 us; the launch traced here: 632 us
  starting transfers between devices  215 us (33%)
  blocking collectives  169 us (26%)
  waiting for transfers between devices  141 us (22%)
  matrix products  58 us (9%)
  between operations  25.2 us (4%)
  local copies, waits for them, and re-layouts  15.8 us (2%)
  other arithmetic  7.94 us (1%)
    psum x2, blocking collectives, on_device(): squares = lax.psum(local_squares, ('rows', 'cols'))  169 us
    ppermute x40, starting transfers between devices, with_halo(): before = lax.ppermute(last, axis, up)  149 us
    ppermute x40, waiting for transfers between devices, with_halo(): after = lax.ppermute(first, axis, down)  134 us
    ppermute x40, starting transfers between devices, with_halo(): after = lax.ppermute(first, axis, down)  66.4 us
    dot_general x72, matrix products, conv_back(): jnp.einsum('oc,ohw->chw', weight[index], window, preferred_element_type=j...  20 us
    dot_general x18, matrix products, render_back(): jnp.einsum('aybx,pyx->pab', window, blocks[index], precision=lax.Precisio...  19.1 us
    dot_general x72, matrix products, conv_forward(): jnp.einsum('oc,chw->ohw', weight[index], window, preferred_element_type=j...  17.7 us
  transfers between devices with their start and end apart: 80, of which 54 were waited for; matrix products, arithmetic and copies ran while one was open for 1% of the time, Pallas kernels for 0%

commit v1 on v0

v1 whole, which is shorter than its diff:
```python
import functools

import jax
import jax.numpy as jnp
import numpy as np
from jax import lax
from jax.experimental import pallas as pl
from jax.experimental.pallas import tpu as pltpu
from jax.sharding import PartitionSpec as P

f32 = jnp.float32
bf16 = jnp.bfloat16
step_rate = 0.25
norm_eps = 1e-06

NP = 6
LAYERS = 4
SIDE = 16
HALF = 8
TR = 32
TC = 128
HALO = 64
WIDE = TC + 2 * HALO
ROWS = TR + 2 * HALO
VMEM_LIMIT = 56 * 1024 * 1024


def iota(shape, dim):
    return lax.broadcasted_iota(jnp.int32, shape, dim)


def split3(x):
    hi = x.astype(bf16)
    rest = x - hi.astype(f32)
    mid = rest.astype(bf16)
    low = (rest - mid.astype(f32)).astype(bf16)
    return hi, mid, low


def dot(a, b):
    return jnp.dot(a, b, preferred_element_type=f32)


def exact_dot(x, ones):
    hi, mid, low = split3(x)
    return dot(hi, ones) + dot(mid, ones) + dot(low, ones)


def lane_fields(width):
    lane = iota((1, width), 1) % 128
    group = lane // 10
    return group, lane - 10 * group, lane < 120


def pack_kernel(film_ref, design_ref, active_ref, target_ref, own_ref, right_ref, left_ref):
    low_half = iota((16, TC), 1) < HALO
    group, spot, used = lane_fields(TC)
    spread = jnp.where(
        (iota((HALF, TC), 0) == spot - 1) & used, 1.0, 0.0
    ).astype(bf16)
    active = active_ref[...].astype(f32)
    row_of = iota((2, TC), 0)
    amp_row = jnp.zeros((1, TC), f32)
    act_row = jnp.zeros((1, TC), f32)
    act_spread = exact_dot(active, spread)
    for p in range(NP):
        mine = row_of + 2 * p == group
        placed = jnp.where(mine, exact_dot(design_ref[p] * active, spread), 0.0)
        amp_row = amp_row + jnp.sum(placed, axis=0, keepdims=True)
        act_row = act_row + jnp.sum(jnp.where(mine, act_spread, 0.0), axis=0, keepdims=True)
    hi, mid, low = split3(amp_row)
    sub = iota((16, TC), 0)
    tile = jnp.where(sub == 0, hi.astype(f32), 0.0)
    tile = jnp.where(sub == 1, mid.astype(f32), tile)
    tile = jnp.where(sub == 2, low.astype(f32), tile)
    tile = jnp.where(sub == 3, act_row, tile).astype(bf16)
    own_ref[0] = tile
    right_ref[19] = tile
    left_ref[19] = tile
    film = jnp.swapaxes(film_ref[...].astype(f32), 0, 1)
    rows = [film[r] for r in range(TR)]
    for piece in split3(target_ref[...]):
        wide = piece.astype(f32)
        rows += [wide[:16], wide[16:]]
    for r, row in enumerate(rows):
        own_ref[1 + r] = row.astype(bf16)
    for r in range(19):
        a, b = rows[r], rows[r + 19]
        right_ref[r] = jnp.where(low_half, pltpu.roll(a, HALO, 1), b).astype(bf16)
        left_ref[r] = jnp.where(low_half, a, pltpu.roll(b, HALO, 1)).astype(bf16)


def widen_kernel(own_ref, from_left_ref, from_right_ref, one_ref, two_ref, three_ref):
    low_half = iota((16, TC), 1) < HALO
    zero = jnp.zeros((16, TC), bf16)
    for out_ref in (one_ref, two_ref, three_ref):
        out_ref[0, :, :TC] = from_left_ref[19]
        out_ref[0, :, TC:] = own_ref[0]
        out_ref[1, :, :TC] = from_right_ref[19]
        out_ref[1, :, TC:] = zero
    for r in range(38):
        own = pltpu.roll(own_ref[1 + r].astype(f32), HALO, 1)
        if r < 19:
            left = from_left_ref[r].astype(f32)
            right = pltpu.roll(from_right_ref[r].astype(f32), HALO, 1)
        else:
            left = pltpu.roll(from_left_ref[r - 19].astype(f32), HALO, 1)
            right = from_right_ref[r - 19].astype(f32)
        first = jnp.where(low_half, left, own).astype(bf16)
        second = jnp.where(low_half, own, right).astype(bf16)
        one_ref[2 + r, :, :TC] = first
        one_ref[2 + r, :, TC:] = second
        if r < TR:
            two_ref[2 + r, :, :TC] = first
            two_ref[2 + r, :, TC:] = second


def combine(gathered):
    own, ring = gathered[:, :128], gathered[:, 128:]
    group, spot, used = lane_fields(128)
    top = (group % 2 == 0) & used
    bottom = (group % 2 == 1) & used
    zero = jnp.zeros((16, 128), f32)
    above = jnp.concatenate([zero, ring[:240]], axis=0)
    below = jnp.concatenate([ring[16:], zero], axis=0)
    summed = own + jnp.where(top, above, 0.0) + jnp.where(bottom, below, 0.0)
    place = iota((256, 128), 0) % 16
    left = jnp.where(place == 0, 0.0, pltpu.roll(summed, 1, 0))
    right = jnp.where(place == 15, 0.0, pltpu.roll(summed, 255, 0))
    left = pltpu.roll(left, 120, 1)
    right = pltpu.roll(right, 8, 1)
    whole = summed + jnp.where(spot == 1, left, 0.0) + jnp.where(spot == 8, right, 0.0)
    whole = jnp.where((spot >= 1) & (spot <= 8) & used, whole, 0.0)
    squares = jnp.sum(jnp.sum(whole * whole, axis=0, keepdims=True), axis=1, keepdims=True)
    lane = iota((1, 128), 1)
    misfits = jnp.sum(
        jnp.where(lane == 120, jnp.sum(own, axis=0, keepdims=True), 0.0), axis=1, keepdims=True
    )
    return whole, squares, misfits


def rate_of(squares, entries):
    return step_rate / jnp.sqrt(squares / entries + norm_eps)


def step_kernel(second, grid, *refs):
    row_count, col_count = grid
    if second:
        (place_ref, dil_ref, vec_ref, wf_ref, wb_ref, stamp_ref, own_ref, u1_ref, u2_ref, u3_ref,
         d1_ref, d2_ref, d3_ref, gathered_ref, out_ref, moved_ref, cat0_ref, cat1_ref, sp_ref, adj_ref,
         height_ref, hg_ref, s2_ref, ampx_ref, acc_ref, whole_ref) = refs
    else:
        (place_ref, dil_ref, vec_ref, wf_ref, wb_ref, stamp_ref, own_ref, u1_ref, u2_ref, u3_ref,
         d1_ref, d2_ref, d3_ref, out_ref, cat0_ref, cat1_ref, sp_ref, adj_ref,
         height_ref, hg_ref, s2_ref, ampx_ref, acc_ref) = refs
    my_row = place_ref[0]
    my_col = place_ref[1]
    group, spot, used = lane_fields(128)
    by_row = [u3_ref, u2_ref, u1_ref, own_ref, d1_ref, d2_ref, d3_ref]

    for k in range(2):
        pick = jnp.where(
            iota((32, WIDE), 0) == (iota((32, WIDE), 1) + HALF) % SIDE + SIDE * k, 1.0, 0.0
        ).astype(bf16)
        s2_ref[k] = exact_dot(stamp_ref[...], pick)

    if second:
        whole, squares, _ = combine(gathered_ref[...])
        whole_ref[...] = whole
        rate = rate_of(squares, float(row_count * col_count * NP * 16))
    masks = iota((16, 384), 0) == jnp.concatenate([group] * 3, axis=1)
    acts = {}
    stacked = []
    for dr in range(-3, 4):
        ref = by_row[dr + 3]
        tiles = [ref[0, :, :TC], ref[0, :, TC:], ref[1, :, :TC]]
        pieces = []
        for dc, tile in zip((-1, 0, 1), tiles):
            t = tile.astype(f32)
            amp = t[0:1] + t[1:2] + t[2:3]
            if second:
                r, c = my_row + dr, my_col + dc
                inside = (r >= 0) & (r < row_count) & (c >= 0) & (c < col_count)
                dev = jnp.where(inside, r * col_count + c, 0)
                moved = rate * whole_ref[pl.ds(dev, 1), :]
                moved = moved * jnp.where(inside, 1.0, 0.0)
                if dr == 0 and dc == 0:
                    moved_ref[...] = moved
                amp = amp - moved
            pieces.append(amp)
            acts[dr, dc] = t[3:4]
        row = jnp.concatenate(pieces, axis=1)
        stacked.append(jnp.where(masks, row, 0.0))
    stacked = jnp.concatenate(stacked, axis=0)
    lane3 = iota((384, WIDE), 0)
    lane1 = lane3 % 128
    spot3 = lane1 % 10
    for k in range(2):
        b = (iota((384, WIDE), 1) + HALF) // SIDE - HALO // SIDE - k
        hit = (b == HALF * (lane3 // 128 - 1) + spot3 - 1) & (spot3 >= 1) & (spot3 <= 8)
        expand = jnp.where(hit & (lane1 < 120), 1.0, 0.0).astype(bf16)
        ampx_ref[k] = exact_dot(stacked, expand)

    for a in range(-4, 6):
        for half in range(2):
            if half == 0:
                terms = ((a, 8), (a - 1, 24))
            else:
                terms = ((a, 16), (a + 1, 0))
            total = jnp.zeros((HALF, WIDE), f32)
            for dimple, first in terms:
                dr, i = dimple // 2, dimple % 2
                for p in range(NP):
                    for k in range(2):
                        row = 16 * (dr + 3) + 2 * p + i
                        total = total + (
                            s2_ref[k, 32 * p + first : 32 * p + first + HALF, :]
                            * ampx_ref[k, row : row + 1, :]
                        )
            start = HALO + SIDE * a + HALF * half
            height_ref[start : start + HALF, :] = total

    col = my_col * TC + iota((16, WIDE), 1) - HALO
    in_map = (col >= 0) & (col < col_count * TC)

    cats = (cat0_ref, cat1_ref)

    def put(slot, b, value, shift):
        cat = cats[slot]
        value = jnp.where(in_map, value, 0.0)
        cat[b, 16:32, :] = value.astype(bf16)
        cat[b, 0:16, :] = pltpu.roll(value, shift, 1).astype(bf16)
        cat[b, 32:48, :] = pltpu.roll(value, WIDE - shift, 1).astype(bf16)

    def wide_row(ref):
        return jnp.broadcast_to(ref, (16, WIDE))

    lift_w = wide_row(vec_ref[0])
    map_lo = jnp.maximum(0, HALO - my_row * TR)
    map_hi = jnp.minimum(ROWS, HALO + (row_count - my_row) * TR)
    d = [dil_ref[l] for l in range(LAYERS)]
    total_d = d[0] + d[1] + d[2] + d[3]

    def round_up(x):
        return (x + 7) // 8 * 8

    def bounds(reach):
        wide = round_up(reach)
        return jnp.maximum(map_lo, HALO - wide), jnp.minimum(map_hi, HALO + TR + wide)

    def over(lo, hi, some_rows):
        count = hi - lo

        def body(step, _):
            some_rows(lo + 32 * step, 32)
            return 0

        full = count // 32
        lax.fori_loop(0, full, body, 0)
        rest = count - 32 * full
        half = rest // 16

        @pl.when(half > 0)
        def _():
            some_rows(lo + 32 * full, 16)

        @pl.when(rest - 16 * half > 0)
        def _():
            some_rows(hi - 8, 8)

    lo0, hi0 = bounds(2 * total_d)
    lift_b = wide_row(vec_ref[1])
    for n, ref in enumerate((u2_ref, u1_ref, own_ref, d1_ref, d2_ref)):
        here = my_row + n - 2
        valid = (here >= 0) & (here < row_count)
        first = jnp.clip(lo0 - n * TR, 0, TR)
        after = jnp.clip(hi0 - n * TR, 0, TR)

        def rows(step, _):
            r0 = first + step * 8
            hs = [height_ref[pl.ds(n * TR + r0 + q, 1), :] for q in range(8)]
            for q in range(8):
                film = ref[2 + r0 + q].astype(f32)
                value = (lift_w * hs[q] + lift_b + film).astype(bf16).astype(f32)
                put(0, n * TR + r0 + q, value, d[0])
            return 0

        lax.fori_loop(0, (after - first) // 8, rows, 0)

        @pl.when(jnp.logical_not(valid))
        def _():
            def blank(r, _):
                cat0_ref[n * TR + r] = jnp.zeros((48, WIDE), bf16)
                cat1_ref[n * TR + r] = jnp.zeros((48, WIDE), bf16)
                return 0

            lax.fori_loop(0, TR, blank, 0)

    def convs(w, slot, b0, n, dil):
        cat = cats[slot]
        out = []
        for q in range(n):
            b = b0 + q
            out.append(dot(w, jnp.concatenate([cat[b - dil], cat[b], cat[b + dil]], axis=0)))
        return out

    def parts(pre):
        s = 0.5 + 0.5 * jnp.tanh(0.5 * pre)
        silu = pre * s
        return silu, s + silu * (1.0 - s)

    reach = 2 * total_d
    for l in range(LAYERS - 1):
        slot = l % 2
        w = wf_ref[l]
        bias = wide_row(vec_ref[3 + l])
        reach = reach - d[l]
        lo, hi = bounds(reach)

        def forward(b0, n):
            pres = convs(w, slot, b0, n, d[l])
            for q in range(n):
                b = b0 + q
                silu, slope = parts(pres[q] + bias)
                sp_ref[l, b] = slope
                value = cats[slot][b, 16:32, :].astype(f32) + silu
                put(1 - slot, b, value.astype(bf16).astype(f32), d[l + 1])

        over(lo, hi, forward)

    for n, ref in enumerate((u1_ref, own_ref, d1_ref)):
        target = ref[34:36].astype(f32) + ref[36:38].astype(f32) + ref[38:40].astype(f32)
        height_ref[TR * (n + 1) : TR * (n + 1) + 16, :] = target[0]
        height_ref[TR * (n + 1) + 16 : TR * (n + 2), :] = target[1]

    acc_ref[...] = jnp.zeros_like(acc_ref)
    lo, hi = bounds(total_d)
    w3 = wf_ref[3]
    bias3 = wide_row(vec_ref[6])
    readout = wide_row(vec_ref[2])

    def turn(b0, n):
        pres = convs(w3, 1, b0, n, d[3])
        targets = [height_ref[pl.ds(b0 + q, 1), :] for q in range(n)]
        for q in range(n):
            b = b0 + q
            silu, slope = parts(pres[q] + bias3)
            value = (cat1_ref[b, 16:32, :].astype(f32) + silu).astype(bf16).astype(f32)
            pressure = jnp.sum(readout * value, axis=0, keepdims=True)
            misfit = pressure - targets[q]
            acc_ref[pl.ds(b, 1), :] = misfit * misfit
            adj = readout * (misfit * (1.0 / (SIDE * SIDE)))
            adj_ref[b] = adj
            put(0, b, (adj * slope).astype(bf16).astype(f32), d[3])

    over(lo, hi, turn)

    reach = total_d
    for l in range(LAYERS - 1, 0, -1):
        slot = (l + 1) % 2
        wb = wb_ref[l]
        reach = reach - d[l]
        lo, hi = bounds(reach)

        def backward(b0, n):
            sums = convs(wb, slot, b0, n, d[l])
            olds = [adj_ref[b0 + q] for q in range(n)]
            for q in range(n):
                b = b0 + q
                adj = olds[q] + sums[q]
                adj_ref[b] = adj
                put(1 - slot, b, (adj * sp_ref[l - 1, b]).astype(bf16).astype(f32), d[l - 1])

        over(lo, hi, backward)

    w0 = wb_ref[0]
    sums = convs(w0, 1, HALO, TR, d[0])
    for q in range(TR):
        adj = adj_ref[HALO + q] + sums[q]
        hg_ref[q : q + 1, :] = jnp.sum(lift_w * adj, axis=0, keepdims=True)

    hg = pltpu.roll(hg_ref[...], WIDE - HALO, 1)[:, :TC]
    spans = {-1: (0, 8, 24), 0: (0, 24, 8), 1: (8, 32, 0), 2: (24, 32, 0)}
    message = []
    for block in ((0, 1), (2, -1)):
        lanes = jnp.zeros((1, TC), f32)
        for k in range(2):
            rows = []
            for p in range(NP):
                for dimple in block:
                    lo_r, hi_r, first = spans[dimple]
                    n = hi_r - lo_r
                    prod = hg[lo_r:hi_r] * s2_ref[k, 32 * p + first : 32 * p + first + n, :TC]
                    rows.append(jnp.sum(prod, axis=0, keepdims=True))
            rows += [jnp.zeros((4, TC), f32)]
            sums = jnp.concatenate(rows, axis=0)
            c = iota((TC, TC), 0)
            gather = jnp.where(((c + HALF) // SIDE - k + 1 == spot) & used, 1.0, 0.0)
            z = exact_dot(sums, gather.astype(bf16))
            lanes = lanes + jnp.sum(
                jnp.where(iota((16, TC), 0) == group, z, 0.0), axis=0, keepdims=True
            )
        message.append(lanes)

    def act_ext(dr):
        act = acts[dr, 0]
        act = act + jnp.where(spot == 0, pltpu.roll(acts[dr, -1], 120, 1), 0.0)
        return act + jnp.where(spot == 9, pltpu.roll(acts[dr, 1], 8, 1), 0.0)

    lane = iota((1, TC), 1)
    own_act = act_ext(0)
    ring_act = jnp.where(group % 2 == 0, act_ext(1), act_ext(-1))
    acc = jnp.sum(acc_ref[HALO : HALO + TR, :], axis=0, keepdims=True)
    inner = (iota((1, WIDE), 1) >= HALO) & (iota((1, WIDE), 1) < HALO + TC)
    local = 0.5 * jnp.sum(jnp.where(inner, acc, 0.0), axis=1, keepdims=True)
    first = jnp.where(used, message[0] * own_act, jnp.where(lane == 120, local, 0.0))
    ring = jnp.where(used, message[1] * ring_act, 0.0)
    out_ref[:, :TC] = first
    out_ref[:, TC:] = ring


def final_kernel(grid, place_ref, design_ref, gathered1_ref, gathered2_ref, moved_ref, new_ref, obj_ref, whole_ref):
    row_count, col_count = grid
    whole, squares, misfit2 = combine(gathered2_ref[...])
    lane = iota((1, 128), 1)
    own = jnp.sum(gathered1_ref[:, :128], axis=0, keepdims=True)
    misfit1 = jnp.sum(jnp.where(lane == 120, own, 0.0), axis=1, keepdims=True)
    whole_ref[...] = whole
    entries = float(row_count * col_count * NP * 16)
    cells = float(row_count * col_count * TR * TC)
    dev = place_ref[0] * col_count + place_ref[1]
    moved = moved_ref[...] + rate_of(squares, entries) * whole_ref[pl.ds(dev, 1), :]
    group, _, _ = lane_fields(128)
    by_group = jnp.where(iota((16, 128), 0) == group, moved, 0.0)
    lanes = iota((128, HALF), 0)
    pick = jnp.where((lanes % 10 == iota((128, HALF), 1) + 1) & (lanes < 120), 1.0, 0.0)
    change = exact_dot(by_group, pick.astype(bf16))
    for p in range(NP):
        new_ref[p] = design_ref[p] - change[2 * p : 2 * p + 2]
    obj_ref[...] = jnp.where(iota((1, 128), 1) == 0, misfit1, misfit2) / cells


def vmem():
    return pl.BlockSpec(memory_space=pltpu.VMEM)


def smem():
    return pl.BlockSpec(memory_space=pltpu.SMEM)


def shape(dims, kind):
    return jax.ShapeDtypeStruct(dims, kind)


def params():
    return pltpu.CompilerParams(vmem_limit_bytes=VMEM_LIMIT)


def on_device(
    row_count, col_count, design, active, stamp_basis, film_field, lift_weight, lift_bias,
    conv_weight, conv_bias, readout, target, dilation,
):
    grid = (row_count, col_count)
    place = jnp.stack([lax.axis_index("rows"), lax.axis_index("cols")]).astype(jnp.int32)
    own, to_right, to_left = pl.pallas_call(
        pack_kernel,
        out_shape=(shape((39, 16, TC), bf16), shape((20, 16, TC), bf16), shape((20, 16, TC), bf16)),
        in_specs=[vmem()] * 4,
        out_specs=(vmem(),) * 3,
        compiler_params=params(),
        name="pack",
    )(film_field, design, active, target)

    def shifted(x, axis, by):
        count = lax.axis_size(axis)
        return lax.ppermute(x, axis, [(i, i + by) for i in range(count) if 0 <= i + by < count])

    from_left = shifted(to_right, "cols", 1)
    from_right = shifted(to_left, "cols", -1)
    one, two, three = pl.pallas_call(
        widen_kernel,
        out_shape=(shape((40, 16, WIDE), bf16), shape((34, 16, WIDE), bf16), shape((2, 16, WIDE), bf16)),
        in_specs=[vmem()] * 3,
        out_specs=(vmem(),) * 3,
        compiler_params=params(),
        name="widen",
    )(own, from_left, from_right)
    u1, d1 = shifted(one, "rows", 1), shifted(one, "rows", -1)
    u2, d2 = shifted(two, "rows", 2), shifted(two, "rows", -2)
    u3, d3 = shifted(three, "rows", 3), shifted(three, "rows", -3)

    wf = jnp.transpose(conv_weight, (0, 2, 1, 3)).reshape(LAYERS, 16, 144)
    wb = jnp.transpose(conv_weight[:, ::-1], (0, 3, 1, 2)).reshape(LAYERS, 16, 144)
    vec = jnp.concatenate(
        [lift_weight[None], lift_bias[None], readout[None], conv_bias], axis=0
    )[:, :, None]
    stamp = stamp_basis.reshape(NP * 32, 32)
    scratch = [
        pltpu.VMEM((ROWS, 48, WIDE), bf16),
        pltpu.VMEM((ROWS, 48, WIDE), bf16),
        pltpu.VMEM((LAYERS - 1, ROWS, 16, WIDE), f32),
        pltpu.VMEM((ROWS, 16, WIDE), f32),
        pltpu.VMEM((ROWS, WIDE), f32),
        pltpu.VMEM((TR, WIDE), f32),
        pltpu.VMEM((2, NP * 32, WIDE), f32),
        pltpu.VMEM((2, 112, WIDE), f32),
        pltpu.VMEM((ROWS, WIDE), f32),
    ]
    common = (place, dilation, vec, wf, wb, stamp, one, u1, u2, u3, d1, d2, d3)
    specs = [smem(), smem()] + [vmem()] * 11

    def gather(message):
        n = row_count * col_count
        spread = jnp.broadcast_to(message[None], (n, 1, 2 * TC))
        return lax.all_to_all(spread, ("rows", "cols"), 0, 0).reshape(n, 2 * TC)

    message1 = pl.pallas_call(
        functools.partial(step_kernel, False, grid),
        out_shape=shape((1, 2 * TC), f32),
        in_specs=specs,
        out_specs=vmem(),
        scratch_shapes=scratch,
        compiler_params=params(),
        name="step_one",
    )(*common)
    gathered1 = gather(message1)
    message2, moved = pl.pallas_call(
        functools.partial(step_kernel, True, grid),
        out_shape=(shape((1, 2 * TC), f32), shape((1, TC), f32)),
        in_specs=specs + [vmem()],
        out_specs=(vmem(), vmem()),
        scratch_shapes=scratch + [pltpu.VMEM((row_count * col_count, TC), f32)],
        compiler_params=params(),
        name="step_two",
    )(*common, gathered1)
    gathered2 = gather(message2)
    new_design, objective = pl.pallas_call(
        functools.partial(final_kernel, grid),
        out_shape=(shape((NP, 2, HALF), f32), shape((1, TC), f32)),
        in_specs=[smem()] + [vmem()] * 4,
        out_specs=(vmem(), vmem()),
        scratch_shapes=[pltpu.VMEM((row_count * col_count, TC), f32)],
        compiler_params=params(),
        name="finish",
    )(place, design, gathered1, gathered2, moved)
    return new_design, objective[0, :2]


def solution(mesh):
    placed = (
        P(None, "rows", "cols"),
        P("rows", "cols"),
        P(),
        P(None, "rows", "cols"),
        P(),
        P(),
        P(),
        P(),
        P(),
        P("rows", "cols"),
        P(),
    )
    return jax.shard_map(
        functools.partial(on_device, mesh.shape["rows"], mesh.shape["cols"]),
        mesh=mesh,
        in_specs=placed,
        out_specs=(P(None, "rows", "cols"), P()),
        check_vma=False,
    )
```

time: 643 us -> 145 us (0.23); the launches traced: 632 us -> 143 us
  starting transfers between devices: 215 us -> 21.7 us
  waiting for transfers between devices: 141 us -> 18.4 us
  blocking collectives: 169 us -> 58.2 us
  matrix products: 58 us -> 0 us
  Pallas kernels: 0 us -> 34.4 us
  between operations: 25.2 us -> 0.85 us
  other arithmetic: 7.94 us -> 0.59 us
  local copies, waits for them, and re-layouts: 15.8 us -> 8.86 us
    ppermute x80 -> x8, starting transfers between devices: 215 us -> 21.7 us  [shifted(): lax.ppermute(x, axis, [(i, i + by) for i in range(count) if 0 <= i + by <...]
    psum x2 -> x0, blocking collectives: 169 us -> none  [on_device(): squares = lax.psum(local_squares, ('rows', 'cols'))]
    ppermute x80 -> x8, waiting for transfers between devices: 141 us -> 18.4 us  [shifted(): lax.ppermute(x, axis, [(i, i + by) for i in range(count) if 0 <= i + by <...]
    all_to_all x0 -> x2, blocking collectives: none -> 58.2 us  [gather(): return lax.all_to_all(spread, ('rows', 'cols'), 0, 0).reshape(n, 2 * TC)]
    dot_general x164 -> x0, matrix products: 58 us -> none  [the longest x72 20 us: conv_back(): jnp.einsum('oc,ohw->chw', weight[index], window, preferred_element_type=j...]
    pallas_call x0 -> x5, Pallas kernels: none -> 34.4 us  [the longest x1 14.3 us: on_device(): pl.pallas_call(functools.partial(step_kernel, True, grid), out_shape=(sha...]
  transfers between devices with their start and end apart: 80 -> 8, of which waited for: 54 -> 2; matrix products, arithmetic and copies ran while one was open for 1% -> 2% of each run, Pallas kernels for 0% -> 0%
where the time goes in v1:
time: 145 us; the launch traced here: 143 us
  blocking collectives  58.2 us (40%)
  Pallas kernels  34.4 us (24%)
  starting transfers between devices  21.7 us (15%)
  waiting for transfers between devices  18.4 us (13%)
  local copies, waits for them, and re-layouts  8.86 us (6%)
    all_to_all x2, blocking collectives, gather(): return lax.all_to_all(spread, ('rows', 'cols'), 0, 0).reshape(n, 2 * TC)  58.2 us
    ppermute x8, starting transfers between devices, shifted(): lax.ppermute(x, axis, [(i, i + by) for i in range(count) if 0 <= i + by <...  21.7 us
    ppermute x8, waiting for transfers between devices, shifted(): lax.ppermute(x, axis, [(i, i + by) for i in range(count) if 0 <= i + by <...  18.4 us
    pallas_call x1, Pallas kernels, on_device(): pl.pallas_call(functools.partial(step_kernel, True, grid), out_shape=(sha...  14.3 us
    pallas_call x1, Pallas kernels, on_device(): pl.pallas_call(functools.partial(step_kernel, False, grid), out_shape=sha...  14.1 us
    unnamed x36, local copies, waits for them, and re-layouts  5.75 us
  transfers between devices with their start and end apart: 8, of which 2 were waited for; matrix products, arithmetic and copies ran while one was open for 2% of the time, Pallas kernels for 0%

profile of v1, /device:TPU:1, one launch (start us, length us, event | category | flops | bytes accessed | tf_op | source)
XLA Modules:
  0.0 143.0 jit_solution(5096212360820535294)
XLA Ops:
  0.6 1.9 %pack.1 = (bf16[39,16,128]{2,1,0:T(8,128)(2,1)}, bf16[20,16,128]{2,1,0:T(8,128)(2,1)}, bf16[20,16,128]{2,1,0:T(8,128)(2,1)}) custom-call(bf16[16,32,128]{2,1,0:T(8,128)(2,1)} %film_ref.1, f32[6,2,8]{2,1,0:T(2,128)} %design_ref.3, s32[2,8]{1,0:T(2,128)} %active_ref.1, f32[32,128]{1,0:T(8,128)} %target_ref.1), custom_call_target="tpu_custom_call" | custom-call | tf_op jit(solution)/shard_map/pack/pallas_call | solution.py:465
  2.5 4.9 %collective-permute-start = (bf16[20,16,128]{2,1,0:T(8,128)(2,1)}, bf16[20,16,128]{2,1,0:T(8,128)(2,1)S(1)}, u32[]{:S(2)}, u32[]{:S(2)}) collective-permute-start(bf16[20,16,128]{2,1,0:T(8,128)(2,1)} %get-tuple-element.13), channel_id=1, source_target_pairs={{0,1},{1,2},{2,3},{3,4},{4,5},{5,6},{6,7},{7,8},{8,9},{9,10},{10,1... | collective-permute-start | bytes 245768 | tf_op jit(solution)/shard_map/ppermute | solution.py:476
  7.4 1.9 %collective-permute-start.1 = (bf16[20,16,128]{2,1,0:T(8,128)(2,1)}, bf16[20,16,128]{2,1,0:T(8,128)(2,1)S(1)}, u32[]{:S(2)}, u32[]{:S(2)}) collective-permute-start(bf16[20,16,128]{2,1,0:T(8,128)(2,1)} %get-tuple-element.14), channel_id=1, source_target_pairs={{1,0},{2,1},{3,2},{4,3},{5,4},{6,5},{7,6},{8,7},{9,8},{10,9},{11,1... | collective-permute-start | bytes 245768 | tf_op jit(solution)/shard_map/ppermute | solution.py:476
  9.4 4.0 %collective-permute-done.1.from_right_ref = bf16[20,16,128]{2,1,0:T(8,128)(2,1)S(1)} collective-permute-done((bf16[20,16,128]{2,1,0:T(8,128)(2,1)}, bf16[20,16,128]{2,1,0:T(8,128)(2,1)S(1)}, u32[]{:S(2)}, u32[]{:S(2)}) %collective-permute-start.1) | collective-permute-done | bytes 81952 | tf_op jit(solution)/shard_map/ppermute | solution.py:476
  13.4 0.6 copy-done.6
  14.0 2.0 %widen.1 = (bf16[40,16,256]{2,1,0:T(8,128)(2,1)}, bf16[34,16,256]{2,1,0:T(8,128)(2,1)}, bf16[2,16,256]{2,1,0:T(8,128)(2,1)}) custom-call(bf16[39,16,128]{2,1,0:T(8,128)(2,1)} %get-tuple-element.12.own_ref, bf16[20,16,128]{2,1,0:T(8,128)(2,1)} %copy-done.5, bf16[20,16,128]{2,1,0:T(8,128)(2,1)} %copy-done.6), custom_call_target="tpu_custom_call" | custom-call | tf_op jit(solution)/shard_map/widen/pallas_call | solution.py:480
  16.1 1.3 collective-permute-start.5
  17.4 4.0 %collective-permute-start.2 = (bf16[40,16,256]{2,1,0:T(8,128)(2,1)}, bf16[40,16,256]{2,1,0:T(8,128)(2,1)S(1)}, u32[]{:S(2)}, u32[]{:S(2)}) collective-permute-start(bf16[40,16,256]{2,1,0:T(8,128)(2,1)} %get-tuple-element.15.refs_6_), channel_id=1, source_target_pairs={{0,16},{16,32},{32,48},{48,64},{64,80},{80,96},{96,112},{112,128},... | collective-permute-start | bytes 983048 | tf_op jit(solution)/shard_map/ppermute | solution.py:476
  21.4 1.3 collective-permute-start.6
  22.7 5.5 %collective-permute-start.3 = (bf16[34,16,256]{2,1,0:T(8,128)(2,1)}, bf16[34,16,256]{2,1,0:T(8,128)(2,1)S(1)}, u32[]{:S(2)}, u32[]{:S(2)}) collective-permute-start(bf16[34,16,256]{2,1,0:T(8,128)(2,1)} %get-tuple-element.16), channel_id=1, source_target_pairs={{0,32},{16,48},{32,64},{48,80},{64,96},{80,112},{96,128},{112,144}... | collective-permute-start | bytes 835592 | tf_op jit(solution)/shard_map/ppermute | solution.py:476
  28.2 1.3 collective-permute-start.7
  29.6 0.6 copy-done.10
  30.2 14.3 %collective-permute-done.7.refs_12_ = bf16[2,16,256]{2,1,0:T(8,128)(2,1)S(1)} collective-permute-done((bf16[2,16,256]{2,1,0:T(8,128)(2,1)}, bf16[2,16,256]{2,1,0:T(8,128)(2,1)S(1)}, u32[]{:S(2)}, u32[]{:S(2)}) %collective-permute-start.7) | collective-permute-done | bytes 16416 | tf_op jit(solution)/shard_map/ppermute | solution.py:476
  44.6 1.5 %collective-permute-start.4 = (bf16[2,16,256]{2,1,0:T(8,128)(2,1)S(1)}, bf16[2,16,256]{2,1,0:T(8,128)(2,1)S(1)}, u32[]{:S(2)}, u32[]{:S(2)}) collective-permute-start(bf16[2,16,256]{2,1,0:T(8,128)(2,1)S(1)} %copy-done.15), channel_id=1, source_target_pairs={{0,48},{16,64},{32,80},{48,96},{64,112},{80,128},{96,144},{112,160... | collective-permute-start | bytes 49160 | tf_op jit(solution)/shard_map/ppermute | solution.py:476
  46.0 0.6 pad_add_fusion.refs_0_.place_ref
  46.6 0.7 copy.25.refs_2_
  47.5 0.7 copy.26.refs_3_
  48.2 0.7 copy.27.refs_4_
  49.0 0.5 copy-done.8
  49.8 0.1 copy-done
  50.0 14.1 %step_one.1 = f32[1,256]{1,0:T(1,128)} custom-call(s32[2]{0:T(128)} %pad_add_fusion.refs_0_.place_ref, s32[4]{0:T(128)} %refs_1_.3, f32[7,16,1]{2,1,0:T(8,128)} %copy.25.refs_2_, bf16[4,16,144]{2,1,0:T(8,128)(2,1)} %copy.26.refs_3_, bf16[4,16,144]{2,1,0:T(8,128)(2,1)} %copy.27.refs_4_, f32[192,32]{1,0:T(8,128)} %bitcast.29, ...), custom_call_target="tpu_custom_call" | custom-call | tf_op jit(solution)/shard_map/step_one/pallas_call | solution.py:517
  64.1 0.7 copy-done.9
  64.8 0.1 broadcast_in_dim.33
  64.9 34.4 %all_to_all.10 = f32[256,1,256]{2,1,0:T(1,128)S(1)} all-to-all(f32[256,1,256]{2,1,0:T(1,128)S(1)} %broadcast_in_dim.33), channel_id=1, replica_groups=mesh['rows'=16,'cols'=16] {'rows','cols'}, dimensions={0} | all-to-all | bytes 524288 | tf_op jit(solution)/shard_map/all_to_all | solution.py:515
  99.4 0.7 copy.36
  100.1 14.3 %step_two.1 = (f32[1,256]{1,0:T(1,128)}, f32[1,128]{1,0:T(1,128)}) custom-call(s32[2]{0:T(128)} %pad_add_fusion.refs_0_.place_ref, s32[4]{0:T(128)} %refs_1_.3, f32[7,16,1]{2,1,0:T(8,128)} %copy.25.refs_2_, bf16[4,16,144]{2,1,0:T(8,128)(2,1)} %copy.26.refs_3_, bf16[4,16,144]{2,1,0:T(8,128)(2,1)} %copy.27.refs_4_, f32[192,32]{1,0:T(8,128)} %bitcast.30, ...), custom_call_target="tpu_custom_call" | custom-call | tf_op jit(solution)/shard_map/step_two/pallas_call | solution.py:527
  114.4 0.7 copy-done.11
  115.2 23.8 %all_to_all.11 = f32[256,1,256]{2,1,0:T(1,128)S(1)} all-to-all(f32[256,1,256]{2,1,0:T(1,128)S(1)} %broadcast_in_dim.35), channel_id=1, replica_groups=mesh['rows'=16,'cols'=16] {'rows','cols'}, dimensions={0} | all-to-all | bytes 524288 | tf_op jit(solution)/shard_map/all_to_all | solution.py:515
  139.0 0.7 copy.35
  139.8 2.0 %finish.1 = (f32[6,2,8]{2,1,0:T(2,128)}, f32[1,128]{1,0:T(1,128)}) custom-call(s32[2]{0:T(128)} %pad_add_fusion.refs_0_.place_ref, f32[6,2,8]{2,1,0:T(2,128)} %design_ref.3, f32[256,256]{1,0:T(8,128)} %bitcast.24, f32[256,256]{1,0:T(8,128)} %bitcast.25, f32[1,128]{1,0:T(1,128)} %get-tuple-element.19.moved_ref), custom_call_target="tpu_custom_call" | custom-call | tf_op jit(solution)/shard_map/finish/pallas_call | solution.py:537
  141.8 0.7 copy-done.16
  142.5 0.5 slice_bitcast_fusion
  (37 shorter events, 0.7 us)
Async XLA Ops:
  2.5 6.9 %collective-permute-start = (bf16[20,16,128]{2,1,0:T(8,128)(2,1)}, bf16[20,16,128]{2,1,0:T(8,128)(2,1)S(1)}, u32[]{:S(2)}, u32[]{:S(2)}) collective-permute-start(bf16[20,16,128]{2,1,0:T(8,128)(2,1)} %get-tuple-element.13), channel_id=1, source_target_pairs={{0,1},{1,2},{2,3},{3,4},{4,5},{5,6},{6,7},{7,8},{8,9},{9,10},{10,1... | collective-permute-start | bytes 245768 | tf_op jit(solution)/shard_map/ppermute | solution.py:476
  7.4 6.0 %collective-permute-start.1 = (bf16[20,16,128]{2,1,0:T(8,128)(2,1)}, bf16[20,16,128]{2,1,0:T(8,128)(2,1)S(1)}, u32[]{:S(2)}, u32[]{:S(2)}) collective-permute-start(bf16[20,16,128]{2,1,0:T(8,128)(2,1)} %get-tuple-element.14), channel_id=1, source_target_pairs={{1,0},{2,1},{3,2},{4,3},{5,4},{6,5},{7,6},{8,7},{9,8},{10,9},{11,1... | collective-permute-start | bytes 245768 | tf_op jit(solution)/shard_map/ppermute | solution.py:476
  9.4 4.0 %copy-start.5 = (bf16[20,16,128]{2,1,0:T(8,128)(2,1)}, bf16[20,16,128]{2,1,0:T(8,128)(2,1)S(1)}, u32[]{:S(2)}) copy-start(bf16[20,16,128]{2,1,0:T(8,128)(2,1)S(1)} %collective-permute-done.from_left_ref) | copy-start | bytes 245764
  13.4 0.6 copy-start.6
  14.0 33.3 %copy-start.4 = (bf16[4,9,16,16]{3,2,1,0:T(8,128)(2,1)S(1)}, bf16[4,9,16,16]{3,2,1,0:T(8,128)(2,1)}, u32[]{:S(2)}) copy-start(bf16[4,9,16,16]{3,2,1,0:T(8,128)(2,1)} %param.17) | copy-start | bytes 55300
  16.1 32.9 %collective-permute-start.5 = (bf16[40,16,256]{2,1,0:T(8,128)(2,1)}, bf16[40,16,256]{2,1,0:T(8,128)(2,1)S(1)}, u32[]{:S(2)}, u32[]{:S(2)}) collective-permute-start(bf16[40,16,256]{2,1,0:T(8,128)(2,1)} %get-tuple-element.15.refs_6_), channel_id=1, source_target_pairs={{16,0},{32,16},{48,32},{64,48},{80,64},{96,80},{112,96},{128,112},... | collective-permute-start | bytes 983048 | tf_op jit(solution)/shard_map/ppermute | solution.py:476
  17.4 31.6 %collective-permute-start.2 = (bf16[40,16,256]{2,1,0:T(8,128)(2,1)}, bf16[40,16,256]{2,1,0:T(8,128)(2,1)S(1)}, u32[]{:S(2)}, u32[]{:S(2)}) collective-permute-start(bf16[40,16,256]{2,1,0:T(8,128)(2,1)} %get-tuple-element.15.refs_6_), channel_id=1, source_target_pairs={{0,16},{16,32},{32,48},{48,64},{64,80},{80,96},{96,112},{112,128},... | collective-permute-start | bytes 983048 | tf_op jit(solution)/shard_map/ppermute | solution.py:476
  21.4 27.6 %collective-permute-start.6 = (bf16[34,16,256]{2,1,0:T(8,128)(2,1)}, bf16[34,16,256]{2,1,0:T(8,128)(2,1)S(1)}, u32[]{:S(2)}, u32[]{:S(2)}) collective-permute-start(bf16[34,16,256]{2,1,0:T(8,128)(2,1)} %get-tuple-element.16), channel_id=1, source_target_pairs={{32,0},{48,16},{64,32},{80,48},{96,64},{112,80},{128,96},{144,112}... | collective-permute-start | bytes 835592 | tf_op jit(solution)/shard_map/ppermute | solution.py:476
  22.7 26.3 %collective-permute-start.3 = (bf16[34,16,256]{2,1,0:T(8,128)(2,1)}, bf16[34,16,256]{2,1,0:T(8,128)(2,1)S(1)}, u32[]{:S(2)}, u32[]{:S(2)}) collective-permute-start(bf16[34,16,256]{2,1,0:T(8,128)(2,1)} %get-tuple-element.16), channel_id=1, source_target_pairs={{0,32},{16,48},{32,64},{48,80},{64,96},{80,112},{96,128},{112,144}... | collective-permute-start | bytes 835592 | tf_op jit(solution)/shard_map/ppermute | solution.py:476
  28.2 16.4 %collective-permute-start.7 = (bf16[2,16,256]{2,1,0:T(8,128)(2,1)}, bf16[2,16,256]{2,1,0:T(8,128)(2,1)S(1)}, u32[]{:S(2)}, u32[]{:S(2)}) collective-permute-start(bf16[2,16,256]{2,1,0:T(8,128)(2,1)} %get-tuple-element.17), channel_id=1, source_target_pairs={{48,0},{64,16},{80,32},{96,48},{112,64},{128,80},{144,96},{160,112... | collective-permute-start | bytes 49160 | tf_op jit(solution)/shard_map/ppermute | solution.py:476
  29.5 0.7 copy-start.10
  29.5 0.7 copy-start.12
  29.5 0.7 copy-start.13
  29.5 0.7 copy-start.14
  29.6 15.0 %copy-start.15 = (bf16[2,16,256]{2,1,0:T(8,128)(2,1)S(1)}, bf16[2,16,256]{2,1,0:T(8,128)(2,1)}, u32[]{:S(2)}) copy-start(bf16[2,16,256]{2,1,0:T(8,128)(2,1)} %get-tuple-element.17) | copy-start | bytes 49156
  44.6 2.8 %copy-start.7 = (bf16[2,16,256]{2,1,0:T(8,128)(2,1)}, bf16[2,16,256]{2,1,0:T(8,128)(2,1)S(1)}, u32[]{:S(2)}) copy-start(bf16[2,16,256]{2,1,0:T(8,128)(2,1)S(1)} %collective-permute-done.7.refs_12_) | copy-start | bytes 49156
  44.6 4.4 %collective-permute-start.4 = (bf16[2,16,256]{2,1,0:T(8,128)(2,1)S(1)}, bf16[2,16,256]{2,1,0:T(8,128)(2,1)S(1)}, u32[]{:S(2)}, u32[]{:S(2)}) collective-permute-start(bf16[2,16,256]{2,1,0:T(8,128)(2,1)S(1)} %copy-done.15), channel_id=1, source_target_pairs={{0,48},{16,64},{32,80},{48,96},{64,112},{80,128},{96,144},{112,160... | collective-permute-start | bytes 49160 | tf_op jit(solution)/shard_map/ppermute | solution.py:476
  49.0 0.6 copy-start.8
  49.0 0.7 copy-start.2
  49.0 0.8 copy-start.3
  49.0 0.9 copy-start
  49.0 1.0 copy-start.1
  64.1 0.7 copy-start.9
  114.4 0.7 copy-start.11
  141.8 0.7 copy-start.16

commit v2 on v1

v2 whole, which is shorter than its diff:
```python
import functools

import jax
import jax.numpy as jnp
import numpy as np
from jax import lax
from jax.experimental import pallas as pl
from jax.experimental.pallas import tpu as pltpu
from jax.sharding import PartitionSpec as P

f32 = jnp.float32
bf16 = jnp.bfloat16
step_rate = 0.25
norm_eps = 1e-06

NP = 6
LAYERS = 4
SIDE = 16
HALF = 8
TR = 32
TC = 128
HALO = 64
WIDE = TC + 2 * HALO
ROWS = TR + 2 * HALO
SPARE = ROWS + 16
PAIRS = 16
MIB = 1024 * 1024


def iota(shape, dim):
    return lax.broadcasted_iota(jnp.int32, shape, dim)


def cell_col(dims):
    lane = iota(dims, 1)
    return jnp.where(lane < TC + HALO, lane, lane - WIDE)


def split3(x):
    hi = x.astype(bf16)
    rest = x - hi.astype(f32)
    mid = rest.astype(bf16)
    low = (rest - mid.astype(f32)).astype(bf16)
    return hi, mid, low


def dot(a, b):
    return jnp.dot(a, b, preferred_element_type=f32)


def exact_dot(x, ones):
    hi, mid, low = split3(x)
    return dot(hi, ones) + dot(mid, ones) + dot(low, ones)


def lane_fields(width):
    lane = iota((1, width), 1) % 128
    group = lane // 10
    return group, lane - 10 * group, lane < 120


def pack_kernel(film_ref, design_ref, active_ref, target_ref, one_ref, up_ref, down_ref):
    group, spot, used = lane_fields(TC)
    spread = jnp.where(
        (iota((HALF, TC), 0) == spot - 1) & used, 1.0, 0.0
    ).astype(bf16)
    active = active_ref[...].astype(f32)
    row_of = iota((2, TC), 0)
    amp_row = jnp.zeros((1, TC), f32)
    act_row = jnp.zeros((1, TC), f32)
    act_spread = exact_dot(active, spread)
    for p in range(NP):
        mine = row_of + 2 * p == group
        placed = jnp.where(mine, exact_dot(design_ref[p] * active, spread), 0.0)
        amp_row = amp_row + jnp.sum(placed, axis=0, keepdims=True)
        act_row = act_row + jnp.sum(jnp.where(mine, act_spread, 0.0), axis=0, keepdims=True)
    hi, mid, low = split3(amp_row)
    sub = iota((16, TC), 0)
    tile = jnp.where(sub == 0, hi.astype(f32), 0.0)
    tile = jnp.where(sub == 1, mid.astype(f32), tile)
    tile = jnp.where(sub == 2, low.astype(f32), tile)
    tile = jnp.where(sub == 3, act_row, tile).astype(bf16)
    one_ref[0] = tile
    up_ref[0] = tile
    down_ref[0] = tile
    film = jnp.swapaxes(film_ref[...].astype(f32), 0, 1).astype(bf16)
    one_ref[1 : 1 + TR] = film
    up_ref[1 : 1 + TR] = film
    down_ref[1 : 1 + TR] = film
    for n, piece in enumerate(split3(target_ref[...])):
        one_ref[33 + 2 * n] = piece[:16]
        one_ref[34 + 2 * n] = piece[16:]


SIDES = 96
AMPS = 89


def tile_pairs(u2, u1, own, d1, d2):
    pairs = [((u2, 1 + r), (u1, 1 + r)) for r in range(TR)]
    pairs += [((own, 1 + r), (own, 17 + r)) for r in range(16)]
    pairs += [((d1, 1 + r), (d2, 1 + r)) for r in range(TR)]
    pairs += [((u1, 33 + r), (d1, 33 + r)) for r in range(6)]
    return pairs + [((own, 33 + r), (own, 36 + r)) for r in range(3)]


def amp_tiles(u2, u1, own, d1, d2):
    return ((u2, 33), (u2, 0), (u1, 0), (own, 0), (d1, 0), (d2, 0), (d2, 33))


def swap_halves(x):
    return pltpu.roll(x, TC // 2, 1)


def halve_kernel(own_ref, u1_ref, u2_ref, d1_ref, d2_ref, right_ref, left_ref):
    low_half = iota((16, TC), 1) < HALO
    pairs = tile_pairs(u2_ref, u1_ref, own_ref, d1_ref, d2_ref)
    for n, ((ref_a, a), (ref_b, b)) in enumerate(pairs):
        first, second = ref_a[a].astype(f32), ref_b[b].astype(f32)
        right_ref[n] = jnp.where(low_half, swap_halves(first), second).astype(bf16)
        left_ref[n] = jnp.where(low_half, first, swap_halves(second)).astype(bf16)
    for n, (ref, at) in enumerate(amp_tiles(u2_ref, u1_ref, own_ref, d1_ref, d2_ref)):
        right_ref[AMPS + n] = ref[at]
        left_ref[AMPS + n] = ref[at]


def combine(gathered):
    own, ring = gathered[:, :128], gathered[:, 128:]
    group, spot, used = lane_fields(128)
    top = (group % 2 == 0) & used
    bottom = (group % 2 == 1) & used
    zero = jnp.zeros((16, 128), f32)
    above = jnp.concatenate([zero, ring[:240]], axis=0)
    below = jnp.concatenate([ring[16:], zero], axis=0)
    summed = own + jnp.where(top, above, 0.0) + jnp.where(bottom, below, 0.0)
    place = iota((256, 128), 0) % 16
    left = jnp.where(place == 0, 0.0, pltpu.roll(summed, 1, 0))
    right = jnp.where(place == 15, 0.0, pltpu.roll(summed, 255, 0))
    left = pltpu.roll(left, 120, 1)
    right = pltpu.roll(right, 8, 1)
    whole = summed + jnp.where(spot == 1, left, 0.0) + jnp.where(spot == 8, right, 0.0)
    whole = jnp.where((spot >= 1) & (spot <= 8) & used, whole, 0.0)
    squares = jnp.sum(jnp.sum(whole * whole, axis=0, keepdims=True), axis=1, keepdims=True)
    lane = iota((1, 128), 1)
    misfits = jnp.sum(
        jnp.where(lane == 120, jnp.sum(own, axis=0, keepdims=True), 0.0), axis=1, keepdims=True
    )
    return whole, squares, misfits


def rate_of(squares, entries):
    return step_rate / jnp.sqrt(squares / entries + norm_eps)


def prep_kernel(stamp_ref, s2_ref, expand_ref):
    for k in range(2):
        pick = jnp.where(
            iota((32, WIDE), 0) == (iota((32, WIDE), 1) + HALF) % SIDE + SIDE * k, 1.0, 0.0
        ).astype(bf16)
        s2_ref[k] = exact_dot(stamp_ref[...], pick)
    lane3 = iota((384, WIDE), 0)
    lane1 = lane3 % 128
    spot3 = lane1 % 10
    for k in range(2):
        b = (cell_col((384, WIDE)) + HALO + HALF) // SIDE - HALO // SIDE - k
        hit = (b == HALF * (lane3 // 128 - 1) + spot3 - 1) & (spot3 >= 1) & (spot3 <= 8)
        expand_ref[k] = jnp.where(hit & (lane1 < 120), 1.0, 0.0).astype(bf16)


def step_kernel(second, grid, *refs):
    row_count, col_count = grid
    (place_ref, dil_ref, vec_ref, wf_ref, wb_ref, s2_ref, expand_ref, own_ref, u1_ref, u2_ref, d1_ref,
     d2_ref, from_left_ref, from_right_ref) = refs[:14]
    rest = refs[14:]
    if second:
        gathered_ref, out_ref, moved_ref, whole_ref = rest[:4]
        rest = rest[4:]
    else:
        out_ref, rest = rest[0], rest[1:]
    cat0_ref, cat1_ref, sp_ref, adj_ref, height_ref, hg_ref, ampx_ref, acc_ref = rest
    my_row = place_ref[0]
    my_col = place_ref[1]
    group, spot, used = lane_fields(128)
    amps = amp_tiles(u2_ref, u1_ref, own_ref, d1_ref, d2_ref)

    if second:
        whole, squares, misfits = combine(gathered_ref[...].reshape(row_count * col_count, 2 * TC))
        whole_ref[...] = whole
        rate = rate_of(squares, float(row_count * col_count * NP * 16))
    masks = iota((16, 384), 0) == jnp.concatenate([group] * 3, axis=1)
    acts = {}
    stacked = []
    for dr in range(-3, 4):
        ref, at = amps[dr + 3]
        tiles = [from_left_ref[AMPS + dr + 3], ref[at], from_right_ref[AMPS + dr + 3]]
        pieces = []
        for dc, tile in zip((-1, 0, 1), tiles):
            t = tile.astype(f32)
            amp = t[0:1] + t[1:2] + t[2:3]
            if second:
                r, c = my_row + dr, my_col + dc
                inside = (r >= 0) & (r < row_count) & (c >= 0) & (c < col_count)
                dev = jnp.where(inside, r * col_count + c, 0)
                moved = rate * whole_ref[pl.ds(dev, 1), :]
                moved = moved * jnp.where(inside, 1.0, 0.0)
                if dr == 0 and dc == 0:
                    moved_ref[...] = jnp.where(iota((1, TC), 1) == 120, misfits, moved)
                amp = amp - moved
            pieces.append(amp)
            acts[dr, dc] = t[3:4]
        row = jnp.concatenate(pieces, axis=1)
        stacked.append(jnp.where(masks, row, 0.0))
    stacked = jnp.concatenate(stacked, axis=0)
    for k in range(2):
        ampx_ref[k] = exact_dot(stacked, expand_ref[k])

    blocks = range(-4, 6)
    for half in range(2):
        totals = [jnp.zeros((HALF, WIDE), f32) for _ in blocks]
        for step, first in ((0, 16 * half if half else 8), (1 if half else -1, 0 if half else 24)):
            for p in range(NP):
                for k in range(2):
                    stamp = s2_ref[k, 32 * p + first : 32 * p + first + HALF, :]
                    for n, a in enumerate(blocks):
                        dr, i = (a + step) // 2, (a + step) % 2
                        row = 16 * (dr + 3) + 2 * p + i
                        totals[n] = totals[n] + stamp * ampx_ref[k, row : row + 1, :]
        for n, a in enumerate(blocks):
            start = HALO + SIDE * a + HALF * half
            height_ref[start : start + HALF, :] = totals[n]

    col = my_col * TC + cell_col((16, WIDE))
    in_map = (col >= 0) & (col < col_count * TC)

    cats = (cat0_ref, cat1_ref)

    def put(slot, b, value, shift):
        cat = cats[slot]
        b = jnp.where(b < map_hi, b, SPARE)
        value = jnp.where(in_map, value, 0.0)
        cat[b, 16:32, :] = value.astype(bf16)
        cat[b, 0:16, :] = pltpu.roll(value, shift, 1).astype(bf16)
        cat[b, 32:48, :] = pltpu.roll(value, WIDE - shift, 1).astype(bf16)

    def wide_row(ref):
        return jnp.broadcast_to(ref, (16, WIDE))

    lift_w = wide_row(vec_ref[0])
    map_lo = jnp.maximum(0, HALO - my_row * TR)
    map_hi = jnp.minimum(ROWS, HALO + (row_count - my_row) * TR)
    d = [dil_ref[l] for l in range(LAYERS)]
    total_d = d[0] + d[1] + d[2] + d[3]

    def bounds(reach):
        return jnp.maximum(map_lo, HALO - reach), jnp.minimum(map_hi, HALO + TR + reach)

    def over(lo, hi, dil, some_pairs):
        count = hi - lo
        whole = count // (2 * dil)
        pairs = whole * dil + jnp.minimum(dil, count - whole * 2 * dil)

        def some(number, base, i):
            firsts = []
            for _ in range(number):
                firsts.append(base + i)
                wrap = i + 1 >= dil
                next_base = jnp.where(wrap, base + 2 * dil, base)
                next_i = jnp.where(wrap, 0, i + 1)
                inside = next_base + next_i < hi
                base = jnp.where(inside, next_base, base)
                i = jnp.where(inside, next_i, i)
            some_pairs(firsts)
            return base, i

        full = pairs // PAIRS
        rest = pairs - PAIRS * full
        full = full + jnp.where(rest > PAIRS // 2, 1, 0)
        base, i = lax.fori_loop(
            0, full, lambda step, at: some(PAIRS, *at), (lo, jnp.int32(0))
        )

        @pl.when((rest > 0) & (rest <= PAIRS // 2))
        def _():
            some(PAIRS // 2, base, i)

    lo0, hi0 = bounds(2 * total_d)
    lift_b = wide_row(vec_ref[1])
    low_half = iota((16, TC), 1) < HALO

    def beside(place, second_row):
        left = from_left_ref[place].astype(f32)
        right = from_right_ref[place].astype(f32)
        if second_row:
            right = swap_halves(right)
        else:
            left = swap_halves(left)
        return jnp.where(low_half, right, left)

    spans = (
        (0, u2_ref, 0, TR, 0, False),
        (1, u1_ref, 0, TR, 0, True),
        (2, own_ref, 0, 16, 32, False),
        (2, own_ref, 16, 16, 32, True),
        (3, d1_ref, 0, TR, 48, False),
        (4, d2_ref, 0, TR, 48, True),
    )
    for n, ref, row0, count, place, second_row in spans:
        here = my_row + n - 2
        valid = (here >= 0) & (here < row_count)
        start = n * TR + row0
        first = jnp.clip(lo0 - start, 0, count)
        after = jnp.clip(hi0 - start, 0, count)

        def rows(step, _):
            r0 = jnp.minimum(first + step * 16, count - 16)
            hs = [height_ref[pl.ds(start + r0 + q, 1), :] for q in range(16)]
            for q in range(16):
                film = jnp.concatenate(
                    [
                        ref[1 + row0 + r0 + q].astype(f32),
                        beside(place + r0 + q, second_row),
                    ],
                    axis=1,
                )
                value = (lift_w * hs[q] + lift_b + film).astype(bf16).astype(f32)
                put(0, start + r0 + q, value, d[0])
            return 0

        lax.fori_loop(0, (after - first + 15) // 16, rows, 0)

        @pl.when(jnp.logical_not(valid))
        def _():
            def blank(r, _):
                cat0_ref[start + r] = jnp.zeros((48, WIDE), bf16)
                cat1_ref[start + r] = jnp.zeros((48, WIDE), bf16)
                return 0

            lax.fori_loop(0, count, blank, 0)

    def convs(w, slot, firsts, dil):
        cat = cats[slot]
        rows, sums = [], []
        for r in firsts:
            near = [cat[r - dil], cat[r], cat[r + dil], cat[r + 2 * dil]]
            both = dot(w, jnp.concatenate(near, axis=0))
            rows += [r, r + dil]
            sums += [both[:16], both[16:]]
        return rows, sums

    def parts(pre):
        s = 0.5 + 0.5 * jnp.tanh(0.5 * pre)
        silu = pre * s
        return silu, s + silu * (1.0 - s)

    reach = 2 * total_d
    for l in range(LAYERS - 1):
        slot = l % 2
        w = wf_ref[l]
        bias = wide_row(vec_ref[3 + l])
        reach = reach - d[l]
        lo, hi = bounds(reach)

        def forward(firsts):
            for b, pre in zip(*convs(w, slot, firsts, d[l])):
                silu, slope = parts(pre + bias)
                sp_ref[l, b] = slope
                value = cats[slot][b, 16:32, :].astype(f32) + silu
                put(1 - slot, b, value.astype(bf16).astype(f32), d[l + 1])

        over(lo, hi, d[l], forward)

    sides = (
        [(80 + r, False) for r in range(6)],
        [(86 + r % 3, r >= 3) for r in range(6)],
        [(80 + r, True) for r in range(6)],
    )
    for n, ref in enumerate((u1_ref, own_ref, d1_ref)):
        for half in range(2):
            target, side = jnp.zeros((16, TC), f32), jnp.zeros((16, TC), f32)
            for piece in (half, half + 2, half + 4):
                target = target + ref[33 + piece].astype(f32)
                side = side + beside(*sides[n][piece])
            first = TR * (n + 1) + 16 * half
            height_ref[first : first + 16, :TC] = target
            height_ref[first : first + 16, TC:] = side

    acc_ref[...] = jnp.zeros_like(acc_ref)
    lo, hi = bounds(total_d)
    w3 = wf_ref[3]
    bias3 = wide_row(vec_ref[6])
    readout = wide_row(vec_ref[2])

    def turn(firsts):
        rows, pres = convs(w3, 1, firsts, d[3])
        targets = [height_ref[pl.ds(b, 1), :] for b in rows]
        for b, pre, target in zip(rows, pres, targets):
            silu, slope = parts(pre + bias3)
            value = (cat1_ref[b, 16:32, :].astype(f32) + silu).astype(bf16).astype(f32)
            pressure = jnp.sum(readout * value, axis=0, keepdims=True)
            misfit = pressure - target
            acc_ref[pl.ds(b, 1), :] = misfit * misfit
            adj = readout * (misfit * (1.0 / (SIDE * SIDE)))
            adj_ref[b] = adj
            put(0, b, (adj * slope).astype(bf16).astype(f32), d[3])

    over(lo, hi, d[3], turn)

    reach = total_d
    for l in range(LAYERS - 1, 0, -1):
        slot = (l + 1) % 2
        wb = wb_ref[l]
        reach = reach - d[l]
        lo, hi = bounds(reach)

        def backward(firsts):
            rows, sums = convs(wb, slot, firsts, d[l])
            olds = [adj_ref[b] for b in rows]
            for b, old, change in zip(rows, olds, sums):
                adj = old + change
                adj_ref[b] = adj
                put(1 - slot, b, (adj * sp_ref[l - 1, b]).astype(bf16).astype(f32), d[l - 1])

        over(lo, hi, d[l], backward)

    w0 = wb_ref[0]

    def last(firsts):
        rows, sums = convs(w0, 1, firsts, d[0])
        for b, change in zip(rows, sums):
            adj = adj_ref[b] + change
            hg_ref[pl.ds(b - HALO, 1), :] = jnp.sum(lift_w * adj, axis=0, keepdims=True)

    over(jnp.int32(HALO), jnp.int32(HALO + TR), d[0], last)

    hg = hg_ref[:TR, :TC]
    spans = {-1: (0, 8, 24), 0: (0, 24, 8), 1: (8, 32, 0), 2: (24, 32, 0)}
    message = []
    for block in ((0, 1), (2, -1)):
        lanes = jnp.zeros((1, TC), f32)
        for k in range(2):
            rows = []
            for p in range(NP):
                for dimple in block:
                    lo_r, hi_r, first = spans[dimple]
                    n = hi_r - lo_r
                    prod = hg[lo_r:hi_r] * s2_ref[k, 32 * p + first : 32 * p + first + n, :TC]
                    rows.append(jnp.sum(prod, axis=0, keepdims=True))
            rows += [jnp.zeros((4, TC), f32)]
            sums = jnp.concatenate(rows, axis=0)
            c = iota((TC, TC), 0)
            gather = jnp.where(((c + HALF) // SIDE - k + 1 == spot) & used, 1.0, 0.0)
            z = exact_dot(sums, gather.astype(bf16))
            lanes = lanes + jnp.sum(
                jnp.where(iota((16, TC), 0) == group, z, 0.0), axis=0, keepdims=True
            )
        message.append(lanes)

    def act_ext(dr):
        act = acts[dr, 0]
        act = act + jnp.where(spot == 0, pltpu.roll(acts[dr, -1], 120, 1), 0.0)
        return act + jnp.where(spot == 9, pltpu.roll(acts[dr, 1], 8, 1), 0.0)

    lane = iota((1, TC), 1)
    own_act = act_ext(0)
    ring_act = jnp.where(group % 2 == 0, act_ext(1), act_ext(-1))
    acc = jnp.sum(acc_ref[HALO : HALO + TR, :], axis=0, keepdims=True)
    local = 0.5 * jnp.sum(acc[:, :TC], axis=1, keepdims=True)
    first = jnp.where(used, message[0] * own_act, jnp.where(lane == 120, local, 0.0))
    ring = jnp.where(used, message[1] * ring_act, 0.0)
    whole_message = jnp.concatenate([first, ring], axis=1)
    out_ref[...] = jnp.broadcast_to(whole_message[None], out_ref.shape)


def final_kernel(grid, place_ref, design_ref, gathered2_ref, moved_ref, new_ref, obj_ref, whole_ref):
    row_count, col_count = grid
    whole, squares, misfit2 = combine(gathered2_ref[...].reshape(row_count * col_count, 2 * TC))
    lane = iota((1, 128), 1)
    whole_ref[...] = whole
    entries = float(row_count * col_count * NP * 16)
    cells = float(row_count * col_count * TR * TC)
    dev = place_ref[0] * col_count + place_ref[1]
    moved = moved_ref[...] + rate_of(squares, entries) * whole_ref[pl.ds(dev, 1), :]
    group, _, _ = lane_fields(128)
    by_group = jnp.where(iota((16, 128), 0) == group, moved, 0.0)
    lanes = iota((128, HALF), 0)
    pick = jnp.where((lanes % 10 == iota((128, HALF), 1) + 1) & (lanes < 120), 1.0, 0.0)
    change = exact_dot(by_group, pick.astype(bf16))
    for p in range(NP):
        new_ref[p] = design_ref[p] - change[2 * p : 2 * p + 2]
    misfit1 = jnp.sum(jnp.where(lane == 120, moved_ref[...], 0.0), axis=1, keepdims=True)
    obj_ref[0] = jnp.sum(misfit1) / cells
    obj_ref[1] = jnp.sum(misfit2) / cells


def vmem():
    return pl.BlockSpec(memory_space=pltpu.VMEM)


def smem():
    return pl.BlockSpec(memory_space=pltpu.SMEM)


def shape(dims, kind):
    return jax.ShapeDtypeStruct(dims, kind)


def params(mib):
    return pltpu.CompilerParams(vmem_limit_bytes=mib * MIB)


def on_device(
    row_count, col_count, design, active, stamp_basis, film_field, lift_weight, lift_bias,
    conv_weight, conv_bias, readout, target, dilation,
):
    grid = (row_count, col_count)
    place = jnp.stack([lax.axis_index("rows"), lax.axis_index("cols")]).astype(jnp.int32)
    one, two_up, two_down = pl.pallas_call(
        pack_kernel,
        out_shape=(shape((39, 16, TC), bf16), shape((34, 16, TC), bf16), shape((34, 16, TC), bf16)),
        in_specs=[vmem()] * 4,
        out_specs=(vmem(),) * 3,
        compiler_params=params(8),
        name="pack",
    )(film_field, design, active, target)

    def shifted(x, axis, by):
        count = lax.axis_size(axis)
        return lax.ppermute(x, axis, [(i, i + by) for i in range(count) if 0 <= i + by < count])

    u1, d1 = shifted(one, "rows", 1), shifted(one, "rows", -1)
    s2, expand = pl.pallas_call(
        prep_kernel,
        out_shape=(shape((2, NP * 32, WIDE), f32), shape((2, 384, WIDE), bf16)),
        in_specs=[vmem()],
        out_specs=(vmem(), vmem()),
        compiler_params=params(8),
        name="prep",
    )(stamp_basis.reshape(NP * 32, 32))
    u1, d1, s2, expand = lax.optimization_barrier((u1, d1, s2, expand))
    u2 = shifted(lax.dynamic_update_slice(two_up, u1[:1], (33, 0, 0)), "rows", 2)
    d2 = shifted(lax.dynamic_update_slice(two_down, d1[:1], (33, 0, 0)), "rows", -2)
    def paired(w):
        return jnp.concatenate(
            [jnp.pad(w, ((0, 0), (0, 0), (0, 48))), jnp.pad(w, ((0, 0), (0, 0), (48, 0)))], axis=1
        )

    wf = jnp.transpose(conv_weight, (0, 2, 1, 3)).reshape(LAYERS, 16, 144)
    wb = jnp.transpose(conv_weight[:, ::-1], (0, 3, 1, 2)).reshape(LAYERS, 16, 144)
    vec = jnp.concatenate(
        [lift_weight[None], lift_bias[None], readout[None], conv_bias], axis=0
    )[:, :, None]
    u2, d2, place = lax.optimization_barrier((u2, d2, place))
    tiles = (one, u1, u2, d1, d2)
    to_right, to_left = pl.pallas_call(
        halve_kernel,
        out_shape=(shape((SIDES, 16, TC), bf16),) * 2,
        in_specs=[vmem()] * 5,
        out_specs=(vmem(),) * 2,
        compiler_params=params(8),
        name="halve",
    )(*tiles)
    from_left = shifted(to_right, "cols", 1)
    from_right = shifted(to_left, "cols", -1)
    scratch = [
        pltpu.VMEM((SPARE + 1, 48, WIDE), bf16),
        pltpu.VMEM((SPARE + 1, 48, WIDE), bf16),
        pltpu.VMEM((LAYERS - 1, ROWS, 16, WIDE), f32),
        pltpu.VMEM((ROWS, 16, WIDE), f32),
        pltpu.VMEM((ROWS, WIDE), f32),
        pltpu.VMEM((TR + HALF, WIDE), f32),
        pltpu.VMEM((2, 112, WIDE), f32),
        pltpu.VMEM((ROWS, WIDE), f32),
    ]
    common = (place, dilation, vec, paired(wf), paired(wb), s2, expand, *tiles, from_left, from_right)
    specs = [smem(), smem()] + [vmem()] * 12

    def gather(message):
        return lax.all_to_all(message, ("rows", "cols"), 0, 0)

    devices = row_count * col_count
    message_shape = shape((devices, 1, 2 * TC), f32)

    message1 = pl.pallas_call(
        functools.partial(step_kernel, False, grid),
        out_shape=message_shape,
        in_specs=specs,
        out_specs=vmem(),
        scratch_shapes=scratch,
        compiler_params=params(30),
        name="step_one",
    )(*common)
    gathered1 = gather(message1)
    message2, moved = pl.pallas_call(
        functools.partial(step_kernel, True, grid),
        out_shape=(message_shape, shape((1, TC), f32)),
        in_specs=specs + [vmem()],
        out_specs=(vmem(), vmem()),
        scratch_shapes=[pltpu.VMEM((devices, TC), f32)] + scratch,
        compiler_params=params(30),
        name="step_two",
    )(*common, gathered1)
    gathered2 = gather(message2)
    new_design, objective = pl.pallas_call(
        functools.partial(final_kernel, grid),
        out_shape=(shape((NP, 2, HALF), f32), shape((2,), f32)),
        in_specs=[smem()] + [vmem()] * 3,
        out_specs=(vmem(), smem()),
        scratch_shapes=[pltpu.VMEM((devices, TC), f32)],
        compiler_params=params(8),
        name="finish",
    )(place, design, gathered2, moved)
    return new_design, objective


def solution(mesh):
    placed = (
        P(None, "rows", "cols"),
        P("rows", "cols"),
        P(),
        P(None, "rows", "cols"),
        P(),
        P(),
        P(),
        P(),
        P(),
        P("rows", "cols"),
        P(),
    )
    return jax.shard_map(
        functools.partial(on_device, mesh.shape["rows"], mesh.shape["cols"]),
        mesh=mesh,
        in_specs=placed,
        out_specs=(P(None, "rows", "cols"), P()),
        check_vma=False,
    )
```

time: 145 us -> 127 us (0.88)
  waiting for transfers between devices: 18.4 us -> 7.82 us
  Pallas kernels: 34.4 us -> 26.5 us
  blocking collectives: 58.2 us -> 62.1 us
  local copies, waits for them, and re-layouts: 8.86 us -> 6.36 us
    ppermute x8 -> x6, waiting for transfers between devices: 18.4 us -> 7.82 us  [shifted(): lax.ppermute(x, axis, [(i, i + by) for i in range(count) if 0 <= i + by <...]
    pallas_call x3 -> x4, Pallas kernels: 30.5 us -> 24.6 us  [the longest x1 12 us: on_device(): pl.pallas_call(functools.partial(step_kernel, True, grid), out_shape=(mes...]
    all_to_all x2, blocking collectives: 58.2 us -> 62.1 us  [gather(): return lax.all_to_all(message, ('rows', 'cols'), 0, 0)]
    pallas_call x1, Pallas kernels: 1.88 us -> 0.24 us  [on_device(): pl.pallas_call(pack_kernel, out_shape=(shape((39, 16, TC), bf16), shape((...]
    unnamed x36 -> x24, local copies, waits for them, and re-layouts: 5.75 us -> 4.33 us
    ppermute x8 -> x6, starting transfers between devices: 21.7 us -> 22 us  [shifted(): lax.ppermute(x, axis, [(i, i + by) for i in range(count) if 0 <= i + by <...]
  transfers between devices with their start and end apart: 8 -> 6, of which waited for: 2 -> 5; matrix products, arithmetic and copies ran while one was open for 2% -> 2% of each run, Pallas kernels for 0% -> 0%
where the time goes in v2:
time: 127 us; the launch traced here: 126 us
  blocking collectives  62.1 us (49%)
  Pallas kernels  26.5 us (21%)
  starting transfers between devices  22 us (17%)
  waiting for transfers between devices  7.82 us (6%)
  local copies, waits for them, and re-layouts  6.36 us (5%)
    all_to_all x2, blocking collectives, gather(): return lax.all_to_all(message, ('rows', 'cols'), 0, 0)  62.1 us
    ppermute x6, starting transfers between devices, shifted(): lax.ppermute(x, axis, [(i, i + by) for i in range(count) if 0 <= i + by <...  22 us
    pallas_call x1, Pallas kernels, on_device(): pl.pallas_call(functools.partial(step_kernel, True, grid), out_shape=(mes...  12 us
    pallas_call x1, Pallas kernels, on_device(): pl.pallas_call(functools.partial(step_kernel, False, grid), out_shape=mes...  11.7 us
    ppermute x6, waiting for transfers between devices, shifted(): lax.ppermute(x, axis, [(i, i + by) for i in range(count) if 0 <= i + by <...  7.82 us
    unnamed x24, local copies, waits for them, and re-layouts  4.33 us
  transfers between devices with their start and end apart: 6, of which 5 were waited for; matrix products, arithmetic and copies ran while one was open for 2% of the time, Pallas kernels for 0%

profile of v2, /device:TPU:1, one launch (start us, length us, event | category | flops | bytes accessed | tf_op | source)
XLA Modules:
  0.0 125.9 jit_solution(1193879686276299346)
XLA Ops:
  0.6 0.9 copy-done
  1.5 0.7 copy-done.2
  2.2 0.7 copy-done.4
  2.9 0.7 copy-done.6
  3.6 0.2 pack.1
  3.9 1.3 %collective-permute-start.1 = (bf16[39,16,128]{2,1,0:T(8,128)(2,1)S(1)}, bf16[39,16,128]{2,1,0:T(8,128)(2,1)S(1)}, u32[]{:S(2)}, u32[]{:S(2)}) collective-permute-start(bf16[39,16,128]{2,1,0:T(8,128)(2,1)S(1)} %get-tuple-element.19.own_ref.refs_7_), channel_id=1, source_target_pairs={{16,0},{32,16},{48,32},{64,48},{80,64},{96,80},{112,96},{128,112},... | collective-permute-start | bytes 479240 | tf_op jit(solution)/shard_map/ppermute | solution.py:528
  5.2 4.6 %collective-permute-start = (bf16[39,16,128]{2,1,0:T(8,128)(2,1)S(1)}, bf16[39,16,128]{2,1,0:T(8,128)(2,1)S(1)}, u32[]{:S(2)}, u32[]{:S(2)}) collective-permute-start(bf16[39,16,128]{2,1,0:T(8,128)(2,1)S(1)} %get-tuple-element.19.own_ref.refs_7_), channel_id=1, source_target_pairs={{0,16},{16,32},{32,48},{48,64},{64,80},{80,96},{96,112},{112,128},... | collective-permute-start | bytes 479240 | tf_op jit(solution)/shard_map/ppermute | solution.py:528
  9.8 0.6 prep.1
  10.3 0.1 collective-permute-done.1.d1_ref.refs_10_
  10.5 1.5 %collective-permute-done.u1_ref.refs_8_ = bf16[39,16,128]{2,1,0:T(8,128)(2,1)S(1)} collective-permute-done((bf16[39,16,128]{2,1,0:T(8,128)(2,1)S(1)}, bf16[39,16,128]{2,1,0:T(8,128)(2,1)S(1)}, u32[]{:S(2)}, u32[]{:S(2)}) %collective-permute-start) | collective-permute-done | bytes 159776 | tf_op jit(solution)/shard_map/ppermute | solution.py:528
  12.0 1.3 %collective-permute-start.3 = (bf16[34,16,128]{2,1,0:T(8,128)(2,1)S(1)}, bf16[34,16,128]{2,1,0:T(8,128)(2,1)S(1)}, u32[]{:S(2)}, u32[]{:S(2)}) collective-permute-start(bf16[34,16,128]{2,1,0:T(8,128)(2,1)S(1)} %slice_dynamic-update-slice_fusion), channel_id=1, source_target_pairs={{32,0},{48,16},{64,32},{80,48},{96,64},{112,80},{128,96},{144,112}... | collective-permute-start | bytes 417800 | tf_op jit(solution)/shard_map/ppermute | solution.py:528
  13.3 6.2 %collective-permute-start.2 = (bf16[34,16,128]{2,1,0:T(8,128)(2,1)S(1)}, bf16[34,16,128]{2,1,0:T(8,128)(2,1)S(1)}, u32[]{:S(2)}, u32[]{:S(2)}) collective-permute-start(bf16[34,16,128]{2,1,0:T(8,128)(2,1)S(1)} %slice_dynamic-update-slice_fusion.1), channel_id=1, source_target_pairs={{0,32},{16,48},{32,64},{48,80},{64,96},{80,112},{96,128},{112,144}... | collective-permute-start | bytes 417800 | tf_op jit(solution)/shard_map/ppermute | solution.py:528
  19.5 0.1 pad_add_fusion.refs_0_.place_ref
  19.6 0.5 collective-permute-done.3.d2_ref.refs_11_
  20.1 1.4 %collective-permute-done.2.u2_ref.refs_9_ = bf16[34,16,128]{2,1,0:T(8,128)(2,1)S(1)} collective-permute-done((bf16[34,16,128]{2,1,0:T(8,128)(2,1)S(1)}, bf16[34,16,128]{2,1,0:T(8,128)(2,1)S(1)}, u32[]{:S(2)}, u32[]{:S(2)}) %collective-permute-start.2) | collective-permute-done | bytes 139296 | tf_op jit(solution)/shard_map/ppermute | solution.py:528
  21.5 0.3 halve.1
  21.8 6.7 %collective-permute-start.4 = (bf16[96,16,128]{2,1,0:T(8,128)(2,1)S(1)}, bf16[96,16,128]{2,1,0:T(8,128)(2,1)S(1)}, u32[]{:S(2)}, u32[]{:S(2)}) collective-permute-start(bf16[96,16,128]{2,1,0:T(8,128)(2,1)S(1)} %get-tuple-element.30), channel_id=1, source_target_pairs={{0,1},{1,2},{2,3},{3,4},{4,5},{5,6},{6,7},{7,8},{8,9},{9,10},{10,1... | collective-permute-start | bytes 1179656 | tf_op jit(solution)/shard_map/ppermute | solution.py:528
  28.5 1.9 %collective-permute-start.5 = (bf16[96,16,128]{2,1,0:T(8,128)(2,1)S(1)}, bf16[96,16,128]{2,1,0:T(8,128)(2,1)S(1)}, u32[]{:S(2)}, u32[]{:S(2)}) collective-permute-start(bf16[96,16,128]{2,1,0:T(8,128)(2,1)S(1)} %get-tuple-element.31), channel_id=1, source_target_pairs={{1,0},{2,1},{3,2},{4,3},{5,4},{6,5},{7,6},{8,7},{9,8},{10,9},{11,1... | collective-permute-start | bytes 1179656 | tf_op jit(solution)/shard_map/ppermute | solution.py:528
  30.5 0.6 copy-done.8
  31.1 0.0 copy-done.11
  31.2 0.1 copy.23.refs_2_
  31.3 0.8 copy.17
  32.1 1.0 copy.18
  33.1 0.1 copy.20
  33.2 0.1 fusion.4
  33.3 4.3 %collective-permute-done.5.refs_13_ = bf16[96,16,128]{2,1,0:T(8,128)(2,1)S(1)} collective-permute-done((bf16[96,16,128]{2,1,0:T(8,128)(2,1)S(1)}, bf16[96,16,128]{2,1,0:T(8,128)(2,1)S(1)}, u32[]{:S(2)}, u32[]{:S(2)}) %collective-permute-start.5) | collective-permute-done | bytes 393248 | tf_op jit(solution)/shard_map/ppermute | solution.py:528
  37.6 0.7 copy-done.5
  38.3 11.7 %step_one.1 = f32[256,1,256]{2,1,0:T(1,128)S(1)} custom-call(s32[2]{0:T(128)S(1)} %pad_add_fusion.refs_0_.place_ref, s32[4]{0:T(128)S(1)} %copy-done.5, f32[7,16,1]{2,1,0:T(8,128)S(1)} %copy.23.refs_2_, bf16[4,32,192]{2,1,0:T(8,128)(2,1)S(1)} %get-tuple-element.34.refs_3_, bf16[4,32,192]{2,1,0:T(8,128)(2,1)S(1)} %get-tuple-element.35.refs_4_, ...), custom_call_target="tpu_custom_call" | custom-call | tf_op jit(solution)/shard_map/step_one/pallas_call | solution.py:583
  50.0 38.5 %all_to_all.10.refs_14_ = f32[256,1,256]{2,1,0:T(1,128)S(1)} all-to-all(f32[256,1,256]{2,1,0:T(1,128)S(1)} %step_one.1), channel_id=1, replica_groups=mesh['rows'=16,'cols'=16] {'rows','cols'}, dimensions={0} | all-to-all | bytes 524288 | tf_op jit(solution)/shard_map/all_to_all | solution.py:578
  88.5 12.0 %step_two.1 = (f32[256,1,256]{2,1,0:T(1,128)S(1)}, f32[1,128]{1,0:T(1,128)S(1)}) custom-call(s32[2]{0:T(128)S(1)} %pad_add_fusion.refs_0_.place_ref, s32[4]{0:T(128)S(1)} %copy-done.5, f32[7,16,1]{2,1,0:T(8,128)S(1)} %copy.23.refs_2_, bf16[4,32,192]{2,1,0:T(8,128)(2,1)S(1)} %get-tuple-element.34.refs_3_, bf16[4,32,192]{2,1,0:T(8,128)(2,1)S(1)} %get-tuple-element.35.refs_4_, ...), custom_call_target="tpu_custom_call" | custom-call | tf_op jit(solution)/shard_map/step_two/pallas_call | solution.py:593
  100.6 23.6 %all_to_all.11.gathered2_ref = f32[256,1,256]{2,1,0:T(1,128)S(1)} all-to-all(f32[256,1,256]{2,1,0:T(1,128)S(1)} %get-tuple-element.32), channel_id=1, replica_groups=mesh['rows'=16,'cols'=16] {'rows','cols'}, dimensions={0} | all-to-all | bytes 524288 | tf_op jit(solution)/shard_map/all_to_all | solution.py:578
  124.2 1.6 %finish.1 = (f32[6,2,8]{2,1,0:T(2,128)}, f32[2]{0:T(128)}) custom-call(s32[2]{0:T(128)S(1)} %pad_add_fusion.refs_0_.place_ref, f32[6,2,8]{2,1,0:T(2,128)S(1)} %copy-done.3, f32[256,1,256]{2,1,0:T(1,128)S(1)} %all_to_all.11.gathered2_ref, f32[1,128]{1,0:T(1,128)S(1)} %get-tuple-element.33.moved_ref), custom_call_target="tpu_custom_call" | custom-call | tf_op jit(solution)/shard_map/finish/pallas_call | solution.py:603
  (22 shorter events, 0.1 us)
Async XLA Ops:
  0.6 0.9 copy-start
  1.5 0.7 copy-start.2
  2.2 0.7 copy-start.4
  2.9 0.7 copy-start.6
  3.6 6.1 %copy-start.1 = (f32[6,32,32]{2,1,0:T(8,128)S(1)}, f32[6,32,32]{2,1,0:T(8,128)}, u32[]{:S(2)}) copy-start(f32[6,32,32]{2,1,0:T(8,128)} %param.13) | copy-start | bytes 73732
  3.9 6.6 %collective-permute-start.1 = (bf16[39,16,128]{2,1,0:T(8,128)(2,1)S(1)}, bf16[39,16,128]{2,1,0:T(8,128)(2,1)S(1)}, u32[]{:S(2)}, u32[]{:S(2)}) collective-permute-start(bf16[39,16,128]{2,1,0:T(8,128)(2,1)S(1)} %get-tuple-element.19.own_ref.refs_7_), channel_id=1, source_target_pairs={{16,0},{32,16},{48,32},{64,48},{80,64},{96,80},{112,96},{128,112},... | collective-permute-start | bytes 479240 | tf_op jit(solution)/shard_map/ppermute | solution.py:528
  5.2 6.8 %collective-permute-start = (bf16[39,16,128]{2,1,0:T(8,128)(2,1)S(1)}, bf16[39,16,128]{2,1,0:T(8,128)(2,1)S(1)}, u32[]{:S(2)}, u32[]{:S(2)}) collective-permute-start(bf16[39,16,128]{2,1,0:T(8,128)(2,1)S(1)} %get-tuple-element.19.own_ref.refs_7_), channel_id=1, source_target_pairs={{0,16},{16,32},{32,48},{48,64},{64,80},{80,96},{96,112},{112,128},... | collective-permute-start | bytes 479240 | tf_op jit(solution)/shard_map/ppermute | solution.py:528
  12.0 8.1 %collective-permute-start.3 = (bf16[34,16,128]{2,1,0:T(8,128)(2,1)S(1)}, bf16[34,16,128]{2,1,0:T(8,128)(2,1)S(1)}, u32[]{:S(2)}, u32[]{:S(2)}) collective-permute-start(bf16[34,16,128]{2,1,0:T(8,128)(2,1)S(1)} %slice_dynamic-update-slice_fusion), channel_id=1, source_target_pairs={{32,0},{48,16},{64,32},{80,48},{96,64},{112,80},{128,96},{144,112}... | collective-permute-start | bytes 417800 | tf_op jit(solution)/shard_map/ppermute | solution.py:528
  13.3 8.2 %collective-permute-start.2 = (bf16[34,16,128]{2,1,0:T(8,128)(2,1)S(1)}, bf16[34,16,128]{2,1,0:T(8,128)(2,1)S(1)}, u32[]{:S(2)}, u32[]{:S(2)}) collective-permute-start(bf16[34,16,128]{2,1,0:T(8,128)(2,1)S(1)} %slice_dynamic-update-slice_fusion.1), channel_id=1, source_target_pairs={{0,32},{16,48},{32,64},{48,80},{64,96},{80,112},{96,128},{112,144}... | collective-permute-start | bytes 417800 | tf_op jit(solution)/shard_map/ppermute | solution.py:528
  21.5 9.8 %copy-start.7 = (bf16[4,9,16,16]{3,2,1,0:T(8,128)(2,1)S(1)}, bf16[4,9,16,16]{3,2,1,0:T(8,128)(2,1)}, u32[]{:S(2)}) copy-start(bf16[4,9,16,16]{3,2,1,0:T(8,128)(2,1)} %param.17) | copy-start | bytes 55300
  21.8 11.5 %collective-permute-start.4 = (bf16[96,16,128]{2,1,0:T(8,128)(2,1)S(1)}, bf16[96,16,128]{2,1,0:T(8,128)(2,1)S(1)}, u32[]{:S(2)}, u32[]{:S(2)}) collective-permute-start(bf16[96,16,128]{2,1,0:T(8,128)(2,1)S(1)} %get-tuple-element.30), channel_id=1, source_target_pairs={{0,1},{1,2},{2,3},{3,4},{4,5},{5,6},{6,7},{7,8},{8,9},{9,10},{10,1... | collective-permute-start | bytes 1179656 | tf_op jit(solution)/shard_map/ppermute | solution.py:528
  28.5 9.1 %collective-permute-start.5 = (bf16[96,16,128]{2,1,0:T(8,128)(2,1)S(1)}, bf16[96,16,128]{2,1,0:T(8,128)(2,1)S(1)}, u32[]{:S(2)}, u32[]{:S(2)}) collective-permute-start(bf16[96,16,128]{2,1,0:T(8,128)(2,1)S(1)} %get-tuple-element.31), channel_id=1, source_target_pairs={{1,0},{2,1},{3,2},{4,3},{5,4},{6,5},{7,6},{8,7},{9,8},{10,9},{11,1... | collective-permute-start | bytes 1179656 | tf_op jit(solution)/shard_map/ppermute | solution.py:528
  30.4 0.7 copy-start.8
  30.4 0.7 copy-start.9
  30.5 0.7 copy-start.10
  30.5 0.7 copy-start.11
  37.6 0.7 copy-start.5
  100.6 23.6 %copy-start.3 = (f32[6,2,8]{2,1,0:T(2,128)S(1)}, f32[6,2,8]{2,1,0:T(2,128)}, u32[]{:S(2)}) copy-start(f32[6,2,8]{2,1,0:T(2,128)} %design_ref.3) | copy-start | bytes 1156

commit v3 on v2

--- a/solution.py
+++ b/solution.py
@@ -59,7 +59,25 @@
     return group, lane - 10 * group, lane < 120
 
 
-def pack_kernel(film_ref, design_ref, active_ref, target_ref, one_ref, up_ref, down_ref):
+def pack_kernel(
+    film_hbm, design_hbm, active_hbm, target_hbm, one_ref, up_ref, down_ref,
+    film_ref, design_ref, active_ref, target_ref, sems,
+):
+    reads = [
+        pltpu.make_async_copy(src, dst, sems.at[n])
+        for n, (src, dst) in enumerate(
+            (
+                (design_hbm, design_ref),
+                (active_hbm, active_ref),
+                (target_hbm, target_ref),
+                (film_hbm, film_ref),
+            )
+        )
+    ]
+    for read in reads:
+        read.start()
+    for read in reads:
+        read.wait()
     group, spot, used = lane_fields(TC)
     spread = jnp.where(
         (iota((HALF, TC), 0) == spot - 1) & used, 1.0, 0.0
@@ -169,9 +187,9 @@
 
 def step_kernel(second, grid, *refs):
     row_count, col_count = grid
-    (place_ref, dil_ref, vec_ref, wf_ref, wb_ref, s2_ref, expand_ref, own_ref, u1_ref, u2_ref, d1_ref,
-     d2_ref, from_left_ref, from_right_ref) = refs[:14]
-    rest = refs[14:]
+    (place_ref, vec_ref, wf_ref, wb_ref, s2_ref, expand_ref, own_ref, u1_ref, u2_ref, d1_ref,
+     d2_ref, from_left_ref, from_right_ref) = refs[:13]
+    rest = refs[13:]
     if second:
         gathered_ref, out_ref, moved_ref, whole_ref = rest[:4]
         rest = rest[4:]
@@ -196,10 +214,11 @@
         pieces = []
         for dc, tile in zip((-1, 0, 1), tiles):
             t = tile.astype(f32)
+            r, c = my_row + dr, my_col + dc
+            inside = (r >= 0) & (r < row_count) & (c >= 0) & (c < col_count)
+            t = t * jnp.where(inside, 1.0, 0.0)
             amp = t[0:1] + t[1:2] + t[2:3]
             if second:
-                r, c = my_row + dr, my_col + dc
-                inside = (r >= 0) & (r < row_count) & (c >= 0) & (c < col_count)
                 dev = jnp.where(inside, r * col_count + c, 0)
                 moved = rate * whole_ref[pl.ds(dev, 1), :]
                 moved = moved * jnp.where(inside, 1.0, 0.0)
@@ -248,7 +267,7 @@
     lift_w = wide_row(vec_ref[0])
     map_lo = jnp.maximum(0, HALO - my_row * TR)
     map_hi = jnp.minimum(ROWS, HALO + (row_count - my_row) * TR)
-    d = [dil_ref[l] for l in range(LAYERS)]
+    d = [place_ref[2 + l] for l in range(LAYERS)]
     total_d = d[0] + d[1] + d[2] + d[3]
 
     def bounds(reach):
@@ -513,19 +532,27 @@
     conv_weight, conv_bias, readout, target, dilation,
 ):
     grid = (row_count, col_count)
-    place = jnp.stack([lax.axis_index("rows"), lax.axis_index("cols")]).astype(jnp.int32)
+    here = jnp.stack([lax.axis_index("rows"), lax.axis_index("cols")]).astype(jnp.int32)
+    place = jnp.concatenate([here, dilation])
     one, two_up, two_down = pl.pallas_call(
         pack_kernel,
         out_shape=(shape((39, 16, TC), bf16), shape((34, 16, TC), bf16), shape((34, 16, TC), bf16)),
-        in_specs=[vmem()] * 4,
+        in_specs=[pl.BlockSpec(memory_space=pltpu.HBM)] * 4,
         out_specs=(vmem(),) * 3,
+        scratch_shapes=[
+            pltpu.VMEM(film_field.shape, bf16),
+            pltpu.VMEM(design.shape, f32),
+            pltpu.VMEM(active.shape, jnp.int32),
+            pltpu.VMEM(target.shape, f32),
+            pltpu.SemaphoreType.DMA((4,)),
+        ],
         compiler_params=params(8),
         name="pack",
-    )(film_field, design, active, target)
+    )(*[pltpu.with_memory_space_constraint(x, pltpu.HBM) for x in (film_field, design, active, target)])
 
     def shifted(x, axis, by):
         count = lax.axis_size(axis)
-        return lax.ppermute(x, axis, [(i, i + by) for i in range(count) if 0 <= i + by < count])
+        return lax.ppermute(x, axis, [(i, (i + by) % count) for i in range(count)])
 
     u1, d1 = shifted(one, "rows", 1), shifted(one, "rows", -1)
     s2, expand = pl.pallas_call(
@@ -571,8 +598,8 @@
         pltpu.VMEM((2, 112, WIDE), f32),
         pltpu.VMEM((ROWS, WIDE), f32),
     ]
-    common = (place, dilation, vec, paired(wf), paired(wb), s2, expand, *tiles, from_left, from_right)
-    specs = [smem(), smem()] + [vmem()] * 12
+    common = (place, vec, paired(wf), paired(wb), s2, expand, *tiles, from_left, from_right)
+    specs = [smem()] + [vmem()] * 12
 
     def gather(message):
         return lax.all_to_all(message, ("rows", "cols"), 0, 0)

time: 127 us -> 112 us (0.88); the launches traced: 126 us -> 112 us
  blocking collectives: 62.1 us -> 51.1 us
  starting transfers between devices: 22 us -> 12.8 us
  waiting for transfers between devices: 7.82 us -> 16.2 us
  local copies, waits for them, and re-layouts: 6.36 us -> 3.4 us
  Pallas kernels: 26.5 us -> 27.9 us
    all_to_all x2, blocking collectives: 62.1 us -> 51.1 us  [gather(): return lax.all_to_all(message, ('rows', 'cols'), 0, 0)]
    ppermute x6, starting transfers between devices: 22 us -> 12.8 us  [shifted(): return lax.ppermute(x, axis, [(i, (i + by) % count) for i in range(count)])]
    ppermute x6, waiting for transfers between devices: 7.82 us -> 16.2 us  [shifted(): return lax.ppermute(x, axis, [(i, (i + by) % count) for i in range(count)])]
    unnamed x24 -> x16, local copies, waits for them, and re-layouts: 4.33 us -> 1.36 us
  transfers between devices with their start and end apart: 6 -> 6, of which waited for: 5 -> 6; matrix products, arithmetic and copies ran while one was open for 2% -> 2% of each run, Pallas kernels for 0% -> 1%
where the time goes in v3:
time: 112 us
  blocking collectives  51.1 us (46%)
  Pallas kernels  27.9 us (25%)
  waiting for transfers between devices  16.2 us (14%)
  starting transfers between devices  12.8 us (11%)
  local copies, waits for them, and re-layouts  3.4 us (3%)
    all_to_all x2, blocking collectives, gather(): return lax.all_to_all(message, ('rows', 'cols'), 0, 0)  51.1 us
    ppermute x6, waiting for transfers between devices, shifted(): return lax.ppermute(x, axis, [(i, (i + by) % count) for i in range(count)])  16.2 us
    ppermute x6, starting transfers between devices, shifted(): return lax.ppermute(x, axis, [(i, (i + by) % count) for i in range(count)])  12.8 us
    pallas_call x1, Pallas kernels, on_device(): pl.pallas_call(functools.partial(step_kernel, True, grid), out_shape=(mes...  12.2 us
    pallas_call x1, Pallas kernels, on_device(): pl.pallas_call(functools.partial(step_kernel, False, grid), out_shape=mes...  12 us
  transfers between devices with their start and end apart: 6, of which 6 were waited for; matrix products, arithmetic and copies ran while one was open for 2% of the time, Pallas kernels for 1%

profile of v3, /device:TPU:1, one launch (start us, length us, event | category | flops | bytes accessed | tf_op | source)
XLA Modules:
  0.0 112.5 jit_solution(16823602761656982537)
XLA Ops:
  0.6 1.3 %pack.1 = (bf16[39,16,128]{2,1,0:T(8,128)(2,1)S(1)}, bf16[34,16,128]{2,1,0:T(8,128)(2,1)S(1)}, bf16[34,16,128]{2,1,0:T(8,128)(2,1)S(1)}) custom-call(bf16[16,32,128]{2,1,0:T(8,128)(2,1)} %film_hbm.1, f32[6,2,8]{2,1,0:T(2,128)} %design_ref.1, s32[2,8]{1,0:T(2,128)} %active_hbm.1, f32[32,128]{1,0:T(8,128)} %target_hbm.1), custom_call_target="tpu_custom_call" | custom-call | tf_op jit(solution)/shard_map/pack/pallas_call | solution.py:537
  1.9 5.8 %collective-permute-start.1 = (bf16[39,16,128]{2,1,0:T(8,128)(2,1)S(1)}, bf16[39,16,128]{2,1,0:T(8,128)(2,1)S(1)}, u32[]{:S(2)}, u32[]{:S(2)}) collective-permute-start(bf16[39,16,128]{2,1,0:T(8,128)(2,1)S(1)} %get-tuple-element.19.own_ref.refs_6_), channel_id=1, source_target_pairs={{0,240},{16,0},{32,16},{48,32},{64,48},{80,64},{96,80},{112,96},{1... | collective-permute-start | bytes 479240 | tf_op jit(solution)/shard_map/ppermute | solution.py:555
  7.8 0.0 collective-permute-start
  7.8 0.6 prep.1
  8.4 2.2 %collective-permute-done.1.d1_ref.refs_9_ = bf16[39,16,128]{2,1,0:T(8,128)(2,1)S(1)} collective-permute-done((bf16[39,16,128]{2,1,0:T(8,128)(2,1)S(1)}, bf16[39,16,128]{2,1,0:T(8,128)(2,1)S(1)}, u32[]{:S(2)}, u32[]{:S(2)}) %collective-permute-start.1) | collective-permute-done | bytes 159776 | tf_op jit(solution)/shard_map/ppermute | solution.py:555
  10.6 5.2 %collective-permute-done.u1_ref.refs_7_ = bf16[39,16,128]{2,1,0:T(8,128)(2,1)S(1)} collective-permute-done((bf16[39,16,128]{2,1,0:T(8,128)(2,1)S(1)}, bf16[39,16,128]{2,1,0:T(8,128)(2,1)S(1)}, u32[]{:S(2)}, u32[]{:S(2)}) %collective-permute-start) | collective-permute-done | bytes 159776 | tf_op jit(solution)/shard_map/ppermute | solution.py:555
  15.8 0.0 collective-permute-start.3
  15.8 3.0 %collective-permute-start.2 = (bf16[34,16,128]{2,1,0:T(8,128)(2,1)S(1)}, bf16[34,16,128]{2,1,0:T(8,128)(2,1)S(1)}, u32[]{:S(2)}, u32[]{:S(2)}) collective-permute-start(bf16[34,16,128]{2,1,0:T(8,128)(2,1)S(1)} %slice_dynamic-update-slice_fusion.1), channel_id=1, source_target_pairs={{0,32},{16,48},{32,64},{48,80},{64,96},{80,112},{96,128},{112,144}... | collective-permute-start | bytes 417800 | tf_op jit(solution)/shard_map/ppermute | solution.py:555
  18.7 0.7 copy-done.4
  19.4 0.1 pad_add_fusion.refs_0_.place_ref
  19.5 1.7 %collective-permute-done.3.d2_ref.refs_10_ = bf16[34,16,128]{2,1,0:T(8,128)(2,1)S(1)} collective-permute-done((bf16[34,16,128]{2,1,0:T(8,128)(2,1)S(1)}, bf16[34,16,128]{2,1,0:T(8,128)(2,1)S(1)}, u32[]{:S(2)}, u32[]{:S(2)}) %collective-permute-start.3) | collective-permute-done | bytes 139296 | tf_op jit(solution)/shard_map/ppermute | solution.py:555
  21.2 2.8 %collective-permute-done.2.u2_ref.refs_8_ = bf16[34,16,128]{2,1,0:T(8,128)(2,1)S(1)} collective-permute-done((bf16[34,16,128]{2,1,0:T(8,128)(2,1)S(1)}, bf16[34,16,128]{2,1,0:T(8,128)(2,1)S(1)}, u32[]{:S(2)}, u32[]{:S(2)}) %collective-permute-start.2) | collective-permute-done | bytes 139296 | tf_op jit(solution)/shard_map/ppermute | solution.py:555
  24.0 0.3 halve.1
  24.3 4.0 %collective-permute-start.4 = (bf16[96,16,128]{2,1,0:T(8,128)(2,1)S(1)}, bf16[96,16,128]{2,1,0:T(8,128)(2,1)S(1)}, u32[]{:S(2)}, u32[]{:S(2)}) collective-permute-start(bf16[96,16,128]{2,1,0:T(8,128)(2,1)S(1)} %get-tuple-element.30), channel_id=1, source_target_pairs={{0,1},{1,2},{2,3},{3,4},{4,5},{5,6},{6,7},{7,8},{8,9},{9,10},{10,1... | collective-permute-start | bytes 1179656 | tf_op jit(solution)/shard_map/ppermute | solution.py:555
  28.2 0.0 collective-permute-start.5
  28.3 0.0 copy-start.7
  28.3 0.7 copy-done.3
  28.9 0.0 copy-done.5
  28.9 0.0 copy-done.7
  29.0 0.1 copy.23.refs_1_
  29.1 0.8 copy.17
  29.9 1.0 copy.18
  30.9 0.1 copy.20
  31.0 0.1 fusion.4
  31.1 1.8 %collective-permute-done.4.refs_11_ = bf16[96,16,128]{2,1,0:T(8,128)(2,1)S(1)} collective-permute-done((bf16[96,16,128]{2,1,0:T(8,128)(2,1)S(1)}, bf16[96,16,128]{2,1,0:T(8,128)(2,1)S(1)}, u32[]{:S(2)}, u32[]{:S(2)}) %collective-permute-start.4) | collective-permute-done | bytes 393248 | tf_op jit(solution)/shard_map/ppermute | solution.py:555
  33.0 2.5 %collective-permute-done.5.refs_12_ = bf16[96,16,128]{2,1,0:T(8,128)(2,1)S(1)} collective-permute-done((bf16[96,16,128]{2,1,0:T(8,128)(2,1)S(1)}, bf16[96,16,128]{2,1,0:T(8,128)(2,1)S(1)}, u32[]{:S(2)}, u32[]{:S(2)}) %collective-permute-start.5) | collective-permute-done | bytes 393248 | tf_op jit(solution)/shard_map/ppermute | solution.py:555
  35.4 12.0 %step_one.1 = f32[256,1,256]{2,1,0:T(1,128)S(1)} custom-call(s32[6]{0:T(128)S(1)} %pad_add_fusion.refs_0_.place_ref, f32[7,16,1]{2,1,0:T(8,128)S(1)} %copy.23.refs_1_, bf16[4,32,192]{2,1,0:T(8,128)(2,1)S(1)} %get-tuple-element.34.refs_2_, bf16[4,32,192]{2,1,0:T(8,128)(2,1)S(1)} %get-tuple-element.35.refs_3_, f32[2,192,256]{2,1,0:T(8,128)S(1)} %get-tuple-element.26.refs_4_, ...), custom_call_target="tpu_custom_call" | custom-call | tf_op jit(solution)/shard_map/step_one/pallas_call | solution.py:610
  47.4 28.1 %all_to_all.10.refs_13_ = f32[256,1,256]{2,1,0:T(1,128)S(1)} all-to-all(f32[256,1,256]{2,1,0:T(1,128)S(1)} %step_one.1), channel_id=1, replica_groups=mesh['rows'=16,'cols'=16] {'rows','cols'}, dimensions={0} | all-to-all | bytes 524288 | tf_op jit(solution)/shard_map/all_to_all | solution.py:605
  75.5 12.2 %step_two.1 = (f32[256,1,256]{2,1,0:T(1,128)S(1)}, f32[1,128]{1,0:T(1,128)S(1)}) custom-call(s32[6]{0:T(128)S(1)} %pad_add_fusion.refs_0_.place_ref, f32[7,16,1]{2,1,0:T(8,128)S(1)} %copy.23.refs_1_, bf16[4,32,192]{2,1,0:T(8,128)(2,1)S(1)} %get-tuple-element.34.refs_2_, bf16[4,32,192]{2,1,0:T(8,128)(2,1)S(1)} %get-tuple-element.35.refs_3_, ...), custom_call_target="tpu_custom_call" | custom-call | tf_op jit(solution)/shard_map/step_two/pallas_call | solution.py:620
  87.7 0.0 copy-start.1
  87.7 23.0 %all_to_all.11.gathered2_ref = f32[256,1,256]{2,1,0:T(1,128)S(1)} all-to-all(f32[256,1,256]{2,1,0:T(1,128)S(1)} %get-tuple-element.32), channel_id=1, replica_groups=mesh['rows'=16,'cols'=16] {'rows','cols'}, dimensions={0} | all-to-all | bytes 524288 | tf_op jit(solution)/shard_map/all_to_all | solution.py:605
  110.7 1.6 %finish.1 = (f32[6,2,8]{2,1,0:T(2,128)}, f32[2]{0:T(128)}) custom-call(s32[6]{0:T(128)S(1)} %pad_add_fusion.refs_0_.place_ref, f32[6,2,8]{2,1,0:T(2,128)S(1)} %copy-done.1, f32[256,1,256]{2,1,0:T(1,128)S(1)} %all_to_all.11.gathered2_ref, f32[1,128]{1,0:T(1,128)S(1)} %get-tuple-element.33.moved_ref), custom_call_target="tpu_custom_call" | custom-call | tf_op jit(solution)/shard_map/finish/pallas_call | solution.py:630
  (14 shorter events, 0.1 us)
Async XLA Ops:
  0.6 7.2 %copy-start = (f32[6,32,32]{2,1,0:T(8,128)S(1)}, f32[6,32,32]{2,1,0:T(8,128)}, u32[]{:S(2)}) copy-start(f32[6,32,32]{2,1,0:T(8,128)} %param.13) | copy-start | bytes 73732
  1.9 8.6 %collective-permute-start.1 = (bf16[39,16,128]{2,1,0:T(8,128)(2,1)S(1)}, bf16[39,16,128]{2,1,0:T(8,128)(2,1)S(1)}, u32[]{:S(2)}, u32[]{:S(2)}) collective-permute-start(bf16[39,16,128]{2,1,0:T(8,128)(2,1)S(1)} %get-tuple-element.19.own_ref.refs_6_), channel_id=1, source_target_pairs={{0,240},{16,0},{32,16},{48,32},{64,48},{80,64},{96,80},{112,96},{1... | collective-permute-start | bytes 479240 | tf_op jit(solution)/shard_map/ppermute | solution.py:555
  7.8 8.0 %collective-permute-start = (bf16[39,16,128]{2,1,0:T(8,128)(2,1)S(1)}, bf16[39,16,128]{2,1,0:T(8,128)(2,1)S(1)}, u32[]{:S(2)}, u32[]{:S(2)}) collective-permute-start(bf16[39,16,128]{2,1,0:T(8,128)(2,1)S(1)} %get-tuple-element.19.own_ref.refs_6_), channel_id=1, source_target_pairs={{0,16},{16,32},{32,48},{48,64},{64,80},{80,96},{96,112},{112,128},... | collective-permute-start | bytes 479240 | tf_op jit(solution)/shard_map/ppermute | solution.py:555
  15.8 5.4 %collective-permute-start.3 = (bf16[34,16,128]{2,1,0:T(8,128)(2,1)S(1)}, bf16[34,16,128]{2,1,0:T(8,128)(2,1)S(1)}, u32[]{:S(2)}, u32[]{:S(2)}) collective-permute-start(bf16[34,16,128]{2,1,0:T(8,128)(2,1)S(1)} %slice_dynamic-update-slice_fusion), channel_id=1, source_target_pairs={{0,224},{16,240},{32,0},{48,16},{64,32},{80,48},{96,64},{112,80},{... | collective-permute-start | bytes 417800 | tf_op jit(solution)/shard_map/ppermute | solution.py:555
  15.8 8.2 %collective-permute-start.2 = (bf16[34,16,128]{2,1,0:T(8,128)(2,1)S(1)}, bf16[34,16,128]{2,1,0:T(8,128)(2,1)S(1)}, u32[]{:S(2)}, u32[]{:S(2)}) collective-permute-start(bf16[34,16,128]{2,1,0:T(8,128)(2,1)S(1)} %slice_dynamic-update-slice_fusion.1), channel_id=1, source_target_pairs={{0,32},{16,48},{32,64},{48,80},{64,96},{80,112},{96,128},{112,144}... | collective-permute-start | bytes 417800 | tf_op jit(solution)/shard_map/ppermute | solution.py:555
  18.7 0.7 copy-start.4
  24.0 5.1 %copy-start.2 = (bf16[4,9,16,16]{3,2,1,0:T(8,128)(2,1)S(1)}, bf16[4,9,16,16]{3,2,1,0:T(8,128)(2,1)}, u32[]{:S(2)}) copy-start(bf16[4,9,16,16]{3,2,1,0:T(8,128)(2,1)} %param.17) | copy-start | bytes 55300
  24.3 8.7 %collective-permute-start.4 = (bf16[96,16,128]{2,1,0:T(8,128)(2,1)S(1)}, bf16[96,16,128]{2,1,0:T(8,128)(2,1)S(1)}, u32[]{:S(2)}, u32[]{:S(2)}) collective-permute-start(bf16[96,16,128]{2,1,0:T(8,128)(2,1)S(1)} %get-tuple-element.30), channel_id=1, source_target_pairs={{0,1},{1,2},{2,3},{3,4},{4,5},{5,6},{6,7},{7,8},{8,9},{9,10},{10,1... | collective-permute-start | bytes 1179656 | tf_op jit(solution)/shard_map/ppermute | solution.py:555
  28.2 7.2 %collective-permute-start.5 = (bf16[96,16,128]{2,1,0:T(8,128)(2,1)S(1)}, bf16[96,16,128]{2,1,0:T(8,128)(2,1)S(1)}, u32[]{:S(2)}, u32[]{:S(2)}) collective-permute-start(bf16[96,16,128]{2,1,0:T(8,128)(2,1)S(1)} %get-tuple-element.31), channel_id=1, source_target_pairs={{0,15},{1,0},{2,1},{3,2},{4,3},{5,4},{6,5},{7,6},{8,7},{9,8},{10,9... | collective-permute-start | bytes 1179656 | tf_op jit(solution)/shard_map/ppermute | solution.py:555
  28.2 0.7 copy-start.3
  28.2 0.7 copy-start.5
  28.2 0.7 copy-start.6
  28.3 0.7 copy-start.7
  87.7 23.0 %copy-start.1 = (f32[6,2,8]{2,1,0:T(2,128)S(1)}, f32[6,2,8]{2,1,0:T(2,128)}, u32[]{:S(2)}) copy-start(f32[6,2,8]{2,1,0:T(2,128)} %design_ref.1) | copy-start | bytes 1156

commit v4 on v3

--- a/solution.py
+++ b/solution.py
@@ -60,7 +60,7 @@
 
 
 def pack_kernel(
-    film_hbm, design_hbm, active_hbm, target_hbm, one_ref, up_ref, down_ref,
+    film_hbm, design_hbm, active_hbm, target_hbm, one_ref, two_ref, three_ref,
     film_ref, design_ref, active_ref, target_ref, sems,
 ):
     reads = [
@@ -99,12 +99,11 @@
     tile = jnp.where(sub == 2, low.astype(f32), tile)
     tile = jnp.where(sub == 3, act_row, tile).astype(bf16)
     one_ref[0] = tile
-    up_ref[0] = tile
-    down_ref[0] = tile
+    two_ref[0] = tile
+    three_ref[0] = tile
     film = jnp.swapaxes(film_ref[...].astype(f32), 0, 1).astype(bf16)
     one_ref[1 : 1 + TR] = film
-    up_ref[1 : 1 + TR] = film
-    down_ref[1 : 1 + TR] = film
+    two_ref[1 : 1 + TR] = film
     for n, piece in enumerate(split3(target_ref[...])):
         one_ref[33 + 2 * n] = piece[:16]
         one_ref[34 + 2 * n] = piece[16:]
@@ -122,22 +121,25 @@
     return pairs + [((own, 33 + r), (own, 36 + r)) for r in range(3)]
 
 
-def amp_tiles(u2, u1, own, d1, d2):
-    return ((u2, 33), (u2, 0), (u1, 0), (own, 0), (d1, 0), (d2, 0), (d2, 33))
+def amp_tiles(u2, u1, own, d1, d2, far):
+    return (far, 0), (u2, 0), (u1, 0), (own, 0), (d1, 0), (d2, 0), (far, 1)
 
 
 def swap_halves(x):
     return pltpu.roll(x, TC // 2, 1)
 
 
-def halve_kernel(own_ref, u1_ref, u2_ref, d1_ref, d2_ref, right_ref, left_ref):
+def halve_kernel(
+    own_ref, u1_ref, u2_ref, d1_ref, d2_ref, far_ref, right_ref, left_ref
+):
     low_half = iota((16, TC), 1) < HALO
     pairs = tile_pairs(u2_ref, u1_ref, own_ref, d1_ref, d2_ref)
     for n, ((ref_a, a), (ref_b, b)) in enumerate(pairs):
         first, second = ref_a[a].astype(f32), ref_b[b].astype(f32)
         right_ref[n] = jnp.where(low_half, swap_halves(first), second).astype(bf16)
         left_ref[n] = jnp.where(low_half, first, swap_halves(second)).astype(bf16)
-    for n, (ref, at) in enumerate(amp_tiles(u2_ref, u1_ref, own_ref, d1_ref, d2_ref)):
+    amps = amp_tiles(u2_ref, u1_ref, own_ref, d1_ref, d2_ref, far_ref)
+    for n, (ref, at) in enumerate(amps):
         right_ref[AMPS + n] = ref[at]
         left_ref[AMPS + n] = ref[at]
 
@@ -187,9 +189,9 @@
 
 def step_kernel(second, grid, *refs):
     row_count, col_count = grid
-    (place_ref, vec_ref, wf_ref, wb_ref, s2_ref, expand_ref, own_ref, u1_ref, u2_ref, d1_ref,
-     d2_ref, from_left_ref, from_right_ref) = refs[:13]
-    rest = refs[13:]
+    (place_ref, vec_ref, wf_ref, wb_ref, s2_ref, expand_ref, own_ref, u1_ref, u2_ref,
+     d1_ref, d2_ref, far_ref, from_left_ref, from_right_ref) = refs[:14]
+    rest = refs[14:]
     if second:
         gathered_ref, out_ref, moved_ref, whole_ref = rest[:4]
         rest = rest[4:]
@@ -199,7 +201,7 @@
     my_row = place_ref[0]
     my_col = place_ref[1]
     group, spot, used = lane_fields(128)
-    amps = amp_tiles(u2_ref, u1_ref, own_ref, d1_ref, d2_ref)
+    amps = amp_tiles(u2_ref, u1_ref, own_ref, d1_ref, d2_ref, far_ref)
 
     if second:
         whole, squares, misfits = combine(gathered_ref[...].reshape(row_count * col_count, 2 * TC))
@@ -534,9 +536,9 @@
     grid = (row_count, col_count)
     here = jnp.stack([lax.axis_index("rows"), lax.axis_index("cols")]).astype(jnp.int32)
     place = jnp.concatenate([here, dilation])
-    one, two_up, two_down = pl.pallas_call(
+    one, two, three = pl.pallas_call(
         pack_kernel,
-        out_shape=(shape((39, 16, TC), bf16), shape((34, 16, TC), bf16), shape((34, 16, TC), bf16)),
+        out_shape=(shape((39, 16, TC), bf16), shape((33, 16, TC), bf16), shape((1, 16, TC), bf16)),
         in_specs=[pl.BlockSpec(memory_space=pltpu.HBM)] * 4,
         out_specs=(vmem(),) * 3,
         scratch_shapes=[
@@ -555,6 +557,8 @@
         return lax.ppermute(x, axis, [(i, (i + by) % count) for i in range(count)])
 
     u1, d1 = shifted(one, "rows", 1), shifted(one, "rows", -1)
+    u2, d2 = shifted(two, "rows", 2), shifted(two, "rows", -2)
+
     s2, expand = pl.pallas_call(
         prep_kernel,
         out_shape=(shape((2, NP * 32, WIDE), f32), shape((2, 384, WIDE), bf16)),
@@ -563,9 +567,16 @@
         compiler_params=params(8),
         name="prep",
     )(stamp_basis.reshape(NP * 32, 32))
-    u1, d1, s2, expand = lax.optimization_barrier((u1, d1, s2, expand))
-    u2 = shifted(lax.dynamic_update_slice(two_up, u1[:1], (33, 0, 0)), "rows", 2)
-    d2 = shifted(lax.dynamic_update_slice(two_down, d1[:1], (33, 0, 0)), "rows", -2)
+    def far(x):
+        return shifted(x, "rows", 3), shifted(x, "rows", -3)
+
+    def near(x):
+        return jnp.zeros_like(x), jnp.zeros_like(x)
+
+    later, s2, expand = lax.optimization_barrier((dilation, s2, expand))
+    amps3 = jnp.concatenate(
+        lax.cond(2 * jnp.sum(later) > HALO - HALF, far, near, three), axis=0
+    )
     def paired(w):
         return jnp.concatenate(
             [jnp.pad(w, ((0, 0), (0, 0), (0, 48))), jnp.pad(w, ((0, 0), (0, 0), (48, 0)))], axis=1
@@ -576,12 +587,12 @@
     vec = jnp.concatenate(
         [lift_weight[None], lift_bias[None], readout[None], conv_bias], axis=0
     )[:, :, None]
-    u2, d2, place = lax.optimization_barrier((u2, d2, place))
-    tiles = (one, u1, u2, d1, d2)
+    u1, d1, u2, d2, amps3, place = lax.optimization_barrier((u1, d1, u2, d2, amps3, place))
+    tiles = (one, u1, u2, d1, d2, amps3)
     to_right, to_left = pl.pallas_call(
         halve_kernel,
         out_shape=(shape((SIDES, 16, TC), bf16),) * 2,
-        in_specs=[vmem()] * 5,
+        in_specs=[vmem()] * 6,
         out_specs=(vmem(),) * 2,
         compiler_params=params(8),
         name="halve",
@@ -599,7 +610,7 @@
         pltpu.VMEM((ROWS, WIDE), f32),
     ]
     common = (place, vec, paired(wf), paired(wb), s2, expand, *tiles, from_left, from_right)
-    specs = [smem()] + [vmem()] * 12
+    specs = [smem()] + [vmem()] * 13
 
     def gather(message):
         return lax.all_to_all(message, ("rows", "cols"), 0, 0)

time: 112 us -> 112 us (level); the launches traced: 112 us -> 110 us
  waiting for transfers between devices: 16.2 us -> 11 us
  blocking collectives: 51.1 us -> 48.3 us
  starting transfers between devices: 12.8 us -> 15.1 us
  other arithmetic: 0.2 us -> 1.55 us
  local copies, waits for them, and re-layouts: 3.4 us -> 4.55 us
    ppermute x6, waiting for transfers between devices: 16.2 us -> 11 us  [shifted(): return lax.ppermute(x, axis, [(i, (i + by) % count) for i in range(count)])]
    all_to_all x2, blocking collectives: 51.1 us -> 48.3 us  [gather(): return lax.all_to_all(message, ('rows', 'cols'), 0, 0)]
    ppermute x6, starting transfers between devices: 12.8 us -> 15.1 us  [shifted(): return lax.ppermute(x, axis, [(i, (i + by) % count) for i in range(count)])]
    another operation x0 -> x2, local copies, waits for them, and re-layouts: none -> 1.19 us
  transfers between devices with their start and end apart: 6 -> 6, of which waited for: 6 -> 4; matrix products, arithmetic and copies ran while one was open for 2% -> 4% of each run, Pallas kernels for 1% -> 1%
where the time goes in v4:
time: 112 us; the launch traced here: 110 us
  blocking collectives  48.3 us (43%)
  Pallas kernels  28.2 us (25%)
  starting transfers between devices  15.1 us (13%)
  waiting for transfers between devices  11 us (10%)
  local copies, waits for them, and re-layouts  4.55 us (4%)
  between operations  1.57 us (1%)
  other arithmetic  1.55 us (1%)
    all_to_all x2, blocking collectives, gather(): return lax.all_to_all(message, ('rows', 'cols'), 0, 0)  48.3 us
    ppermute x6, starting transfers between devices, shifted(): return lax.ppermute(x, axis, [(i, (i + by) % count) for i in range(count)])  15.1 us
    pallas_call x1, Pallas kernels, on_device(): pl.pallas_call(functools.partial(step_kernel, True, grid), out_shape=(mes...  12.4 us
    pallas_call x1, Pallas kernels, on_device(): pl.pallas_call(functools.partial(step_kernel, False, grid), out_shape=mes...  12 us
    ppermute x6, waiting for transfers between devices, shifted(): return lax.ppermute(x, axis, [(i, (i + by) % count) for i in range(count)])  11 us
  transfers between devices with their start and end apart: 6, of which 4 were waited for; matrix products, arithmetic and copies ran while one was open for 4% of the time, Pallas kernels for 1%

profile of v4, /device:TPU:1, one launch (start us, length us, event | category | flops | bytes accessed | tf_op | source)
XLA Modules:
  0.0 110.3 jit_solution(12013439673444476759)
XLA Ops:
  0.6 1.3 %pack.1 = (bf16[39,16,128]{2,1,0:T(8,128)(2,1)S(1)}, bf16[33,16,128]{2,1,0:T(8,128)(2,1)S(1)}, bf16[1,16,128]{2,1,0:T(8,128)(2,1)S(1)}) custom-call(bf16[16,32,128]{2,1,0:T(8,128)(2,1)} %film_hbm.1, f32[6,2,8]{2,1,0:T(2,128)} %design_ref.1, s32[2,8]{1,0:T(2,128)} %active_hbm.1, f32[32,128]{1,0:T(8,128)} %target_hbm.1), custom_call_target="tpu_custom_call" | custom-call | tf_op jit(solution)/shard_map/pack/pallas_call | solution.py:539
  1.9 6.1 %collective-permute-start.5 = (bf16[33,16,128]{2,1,0:T(8,128)(2,1)S(1)}, bf16[33,16,128]{2,1,0:T(8,128)(2,1)S(1)}, u32[]{:S(2)}, u32[]{:S(2)}) collective-permute-start(bf16[33,16,128]{2,1,0:T(8,128)(2,1)S(1)} %get-tuple-element.24), channel_id=1, source_target_pairs={{0,224},{16,240},{32,0},{48,16},{64,32},{80,48},{96,64},{112,80},{... | collective-permute-start | bytes 405512 | tf_op jit(solution)/shard_map/ppermute | solution.py:557
  8.1 4.8 %collective-permute-start.3 = (bf16[39,16,128]{2,1,0:T(8,128)(2,1)S(1)}, bf16[39,16,128]{2,1,0:T(8,128)(2,1)S(1)}, u32[]{:S(2)}, u32[]{:S(2)}) collective-permute-start(bf16[39,16,128]{2,1,0:T(8,128)(2,1)S(1)} %get-tuple-element.23.own_ref.refs_6_), channel_id=1, source_target_pairs={{0,240},{16,0},{32,16},{48,32},{64,48},{80,64},{96,80},{112,96},{1... | collective-permute-start | bytes 479240 | tf_op jit(solution)/shard_map/ppermute | solution.py:557
  12.9 0.6 prep.1
  13.4 0.0 copy-start.4
  13.4 0.6 copy-done.4
  14.1 0.6 reduce_sum.9
  15.4 1.2 %conditional.1 = (bf16[1,16,128]{2,1,0:T(8,128)(2,1)}, bf16[1,16,128]{2,1,0:T(8,128)(2,1)}) conditional(s32[]{:T(128)} %convert_element_type.9, () %tuple.18, bf16[1,16,128]{2,1,0:T(8,128)(2,1)S(1)} %get-tuple-element.28), branch_computations={%region_1.0_spmd, %region_2.0_spmd} | conditional | bytes 32864 | solution.py:578
  15.4 0.6 broadcast.2.clone
  16.0 0.6 broadcast.2
  16.6 0.1 pad_add_fusion.refs_0_.place_ref
  16.7 0.7 pad_maximum_fusion.far_ref.refs_11_
  17.4 0.3 collective-permute-done.3.d1_ref.refs_9_
  17.7 6.4 %collective-permute-done.2.u1_ref.refs_7_ = bf16[39,16,128]{2,1,0:T(8,128)(2,1)S(1)} collective-permute-done((bf16[39,16,128]{2,1,0:T(8,128)(2,1)S(1)}, bf16[39,16,128]{2,1,0:T(8,128)(2,1)S(1)}, u32[]{:S(2)}, u32[]{:S(2)}) %collective-permute-start.2) | collective-permute-done | bytes 159776 | tf_op jit(solution)/shard_map/ppermute | solution.py:557
  24.0 0.3 halve.1
  24.3 4.2 %collective-permute-start.6 = (bf16[96,16,128]{2,1,0:T(8,128)(2,1)S(1)}, bf16[96,16,128]{2,1,0:T(8,128)(2,1)S(1)}, u32[]{:S(2)}, u32[]{:S(2)}) collective-permute-start(bf16[96,16,128]{2,1,0:T(8,128)(2,1)S(1)} %get-tuple-element.39), channel_id=1, source_target_pairs={{0,1},{1,2},{2,3},{3,4},{4,5},{5,6},{6,7},{7,8},{8,9},{9,10},{10,1... | collective-permute-start | bytes 1179656 | tf_op jit(solution)/shard_map/ppermute | solution.py:557
  28.6 0.0 copy-start.7
  28.6 0.7 copy-done.3
  29.2 0.0 copy-done.7
  29.3 0.1 copy.23.refs_1_
  29.4 0.8 copy.17
  30.2 1.0 copy.18
  31.2 0.1 copy.20
  31.3 0.1 fusion.4
  31.4 1.9 %collective-permute-done.6.refs_12_ = bf16[96,16,128]{2,1,0:T(8,128)(2,1)S(1)} collective-permute-done((bf16[96,16,128]{2,1,0:T(8,128)(2,1)S(1)}, bf16[96,16,128]{2,1,0:T(8,128)(2,1)S(1)}, u32[]{:S(2)}, u32[]{:S(2)}) %collective-permute-start.6) | collective-permute-done | bytes 393248 | tf_op jit(solution)/shard_map/ppermute | solution.py:557
  33.3 2.5 %collective-permute-done.7.refs_13_ = bf16[96,16,128]{2,1,0:T(8,128)(2,1)S(1)} collective-permute-done((bf16[96,16,128]{2,1,0:T(8,128)(2,1)S(1)}, bf16[96,16,128]{2,1,0:T(8,128)(2,1)S(1)}, u32[]{:S(2)}, u32[]{:S(2)}) %collective-permute-start.7) | collective-permute-done | bytes 393248 | tf_op jit(solution)/shard_map/ppermute | solution.py:557
  35.8 12.0 %step_one.1 = f32[256,1,256]{2,1,0:T(1,128)S(1)} custom-call(s32[6]{0:T(128)S(1)} %pad_add_fusion.refs_0_.place_ref, f32[7,16,1]{2,1,0:T(8,128)S(1)} %copy.23.refs_1_, bf16[4,32,192]{2,1,0:T(8,128)(2,1)S(1)} %get-tuple-element.43.refs_2_, bf16[4,32,192]{2,1,0:T(8,128)(2,1)S(1)} %get-tuple-element.44.refs_3_, f32[2,192,256]{2,1,0:T(8,128)S(1)} %get-tuple-element.32.refs_4_, ...), custom_call_target="tpu_custom_call" | custom-call | tf_op jit(solution)/shard_map/step_one/pallas_call | solution.py:621
  47.8 25.2 %all_to_all.10.refs_14_ = f32[256,1,256]{2,1,0:T(1,128)S(1)} all-to-all(f32[256,1,256]{2,1,0:T(1,128)S(1)} %step_one.1), channel_id=1, replica_groups=mesh['rows'=16,'cols'=16] {'rows','cols'}, dimensions={0} | all-to-all | bytes 524288 | tf_op jit(solution)/shard_map/all_to_all | solution.py:616
  72.9 12.4 %step_two.1 = (f32[256,1,256]{2,1,0:T(1,128)S(1)}, f32[1,128]{1,0:T(1,128)S(1)}) custom-call(s32[6]{0:T(128)S(1)} %pad_add_fusion.refs_0_.place_ref, f32[7,16,1]{2,1,0:T(8,128)S(1)} %copy.23.refs_1_, bf16[4,32,192]{2,1,0:T(8,128)(2,1)S(1)} %get-tuple-element.43.refs_2_, bf16[4,32,192]{2,1,0:T(8,128)(2,1)S(1)} %get-tuple-element.44.refs_3_, ...), custom_call_target="tpu_custom_call" | custom-call | tf_op jit(solution)/shard_map/step_two/pallas_call | solution.py:631
  85.3 0.0 copy-start.1
  85.3 23.2 %all_to_all.11.gathered2_ref = f32[256,1,256]{2,1,0:T(1,128)S(1)} all-to-all(f32[256,1,256]{2,1,0:T(1,128)S(1)} %get-tuple-element.41), channel_id=1, replica_groups=mesh['rows'=16,'cols'=16] {'rows','cols'}, dimensions={0} | all-to-all | bytes 524288 | tf_op jit(solution)/shard_map/all_to_all | solution.py:616
  108.5 1.6 %finish.1 = (f32[6,2,8]{2,1,0:T(2,128)}, f32[2]{0:T(128)}) custom-call(s32[6]{0:T(128)S(1)} %pad_add_fusion.refs_0_.place_ref, f32[6,2,8]{2,1,0:T(2,128)S(1)} %copy-done.1, f32[256,1,256]{2,1,0:T(1,128)S(1)} %all_to_all.11.gathered2_ref, f32[1,128]{1,0:T(1,128)S(1)} %get-tuple-element.42.moved_ref), custom_call_target="tpu_custom_call" | custom-call | tf_op jit(solution)/shard_map/finish/pallas_call | solution.py:641
  (17 shorter events, 0.1 us)
Async XLA Ops:
  0.6 12.2 %copy-start = (f32[6,32,32]{2,1,0:T(8,128)S(1)}, f32[6,32,32]{2,1,0:T(8,128)}, u32[]{:S(2)}) copy-start(f32[6,32,32]{2,1,0:T(8,128)} %param.15) | copy-start | bytes 73732
  1.9 15.4 %collective-permute-start.5 = (bf16[33,16,128]{2,1,0:T(8,128)(2,1)S(1)}, bf16[33,16,128]{2,1,0:T(8,128)(2,1)S(1)}, u32[]{:S(2)}, u32[]{:S(2)}) collective-permute-start(bf16[33,16,128]{2,1,0:T(8,128)(2,1)S(1)} %get-tuple-element.24), channel_id=1, source_target_pairs={{0,224},{16,240},{32,0},{48,16},{64,32},{80,48},{96,64},{112,80},{... | collective-permute-start | bytes 405512 | tf_op jit(solution)/shard_map/ppermute | solution.py:557
  8.0 9.3 %collective-permute-start.4 = (bf16[33,16,128]{2,1,0:T(8,128)(2,1)S(1)}, bf16[33,16,128]{2,1,0:T(8,128)(2,1)S(1)}, u32[]{:S(2)}, u32[]{:S(2)}) collective-permute-start(bf16[33,16,128]{2,1,0:T(8,128)(2,1)S(1)} %get-tuple-element.24), channel_id=1, source_target_pairs={{0,32},{16,48},{32,64},{48,80},{64,96},{80,112},{96,128},{112,144}... | collective-permute-start | bytes 405512 | tf_op jit(solution)/shard_map/ppermute | solution.py:557
  8.1 9.6 %collective-permute-start.3 = (bf16[39,16,128]{2,1,0:T(8,128)(2,1)S(1)}, bf16[39,16,128]{2,1,0:T(8,128)(2,1)S(1)}, u32[]{:S(2)}, u32[]{:S(2)}) collective-permute-start(bf16[39,16,128]{2,1,0:T(8,128)(2,1)S(1)} %get-tuple-element.23.own_ref.refs_6_), channel_id=1, source_target_pairs={{0,240},{16,0},{32,16},{48,32},{64,48},{80,64},{96,80},{112,96},{1... | collective-permute-start | bytes 479240 | tf_op jit(solution)/shard_map/ppermute | solution.py:557
  13.4 0.7 copy-start.4
  16.6 7.4 %collective-permute-start.2 = (bf16[39,16,128]{2,1,0:T(8,128)(2,1)S(1)}, bf16[39,16,128]{2,1,0:T(8,128)(2,1)S(1)}, u32[]{:S(2)}, u32[]{:S(2)}) collective-permute-start(bf16[39,16,128]{2,1,0:T(8,128)(2,1)S(1)} %get-tuple-element.23.own_ref.refs_6_), channel_id=1, source_target_pairs={{0,16},{16,32},{32,48},{48,64},{64,80},{80,96},{96,112},{112,128},... | collective-permute-start | bytes 479240 | tf_op jit(solution)/shard_map/ppermute | solution.py:557
  24.0 5.4 %copy-start.2 = (bf16[4,9,16,16]{3,2,1,0:T(8,128)(2,1)S(1)}, bf16[4,9,16,16]{3,2,1,0:T(8,128)(2,1)}, u32[]{:S(2)}) copy-start(bf16[4,9,16,16]{3,2,1,0:T(8,128)(2,1)} %param.19) | copy-start | bytes 55300
  24.3 8.9 %collective-permute-start.6 = (bf16[96,16,128]{2,1,0:T(8,128)(2,1)S(1)}, bf16[96,16,128]{2,1,0:T(8,128)(2,1)S(1)}, u32[]{:S(2)}, u32[]{:S(2)}) collective-permute-start(bf16[96,16,128]{2,1,0:T(8,128)(2,1)S(1)} %get-tuple-element.39), channel_id=1, source_target_pairs={{0,1},{1,2},{2,3},{3,4},{4,5},{5,6},{6,7},{7,8},{8,9},{9,10},{10,1... | collective-permute-start | bytes 1179656 | tf_op jit(solution)/shard_map/ppermute | solution.py:557
  28.5 7.2 %collective-permute-start.7 = (bf16[96,16,128]{2,1,0:T(8,128)(2,1)S(1)}, bf16[96,16,128]{2,1,0:T(8,128)(2,1)S(1)}, u32[]{:S(2)}, u32[]{:S(2)}) collective-permute-start(bf16[96,16,128]{2,1,0:T(8,128)(2,1)S(1)} %get-tuple-element.40), channel_id=1, source_target_pairs={{0,15},{1,0},{2,1},{3,2},{4,3},{5,4},{6,5},{7,6},{8,7},{9,8},{10,9... | collective-permute-start | bytes 1179656 | tf_op jit(solution)/shard_map/ppermute | solution.py:557
  28.6 0.7 copy-start.3
  28.6 0.7 copy-start.5
  28.6 0.7 copy-start.6
  28.6 0.7 copy-start.7
  85.3 23.2 %copy-start.1 = (f32[6,2,8]{2,1,0:T(2,128)S(1)}, f32[6,2,8]{2,1,0:T(2,128)}, u32[]{:S(2)}) copy-start(f32[6,2,8]{2,1,0:T(2,128)} %design_ref.1) | copy-start | bytes 1156
